TPU v7x, 512 devices: a whole 4x4x16 slice. The times are simulated.
512 devices in a mesh: occ: 16 (over x_hi, y, core), vir: 32 (over z, x_lo).
Axes of the slice: x: 4 (x_hi: 2, x_lo: 2; x = x_hi * 2 + x_lo), y: 4, z: 16, core: 2. Of those that a mesh axis runs over, the one named last changes fastest.
Arguments:
- orbitals: bfloat16 [16, 8192, 4096], P('occ', 'vir'), may hold values from -0.75 to 0.75
- eps_occ: bfloat16 [16], P('occ'), may hold values from -2.5 to -0.5
- eps_vir: bfloat16 [8192], P('vir'), may hold values from 0.5 to 3
Outputs:
- density: bfloat16 [16, 8192, 4096], P('occ', 'vir')
All inputs are finite; a program needn't handle non-finite values.
Results may differ from a plain program's by a relative error of at most 0.0047.
Values may be sent and summed in bfloat16 or wider, within the bound.
No kernel may reach another device: no remote copies, remote signals or barrier semaphores. Data moves between devices by JAX's collectives and lax.ppermute only.
A program may use at most 64 MiB of HBM per device.

v0:
```python
import jax
import jax.numpy as jnp
from jax import lax
from jax.sharding import PartitionSpec as P

BATCH_DEV = 8
REACH = 1


def shifted_2(block, axis, distance):
    devices = range(lax.axis_size(axis))
    route = [((i - distance) % len(devices), i) for i in devices]
    return lax.ppermute(block, axis, route)


def pair_energies(eps_occ, occ_stack, eps_vir, batch_energy):
    own_energy = eps_occ.astype(jnp.float32)
    others = occ_stack.astype(jnp.float32)
    vir_energy = eps_vir.astype(jnp.float32)
    batch_virt = batch_energy.astype(jnp.float32)
    return (
        vir_energy[None, :, None, None, None]
        + batch_virt[None, None, None, None, :]
        - own_energy[:, None, None, None, None]
        - others[None, None, :, :, None]
    )


def shards(orbitals, eps_occ, eps_vir):
    occ_dev, vir_dev, aux_width = orbitals.shape
    block_count = 2 * REACH + 1
    offsets = list(range(-REACH, REACH + 1))
    resident = orbitals.reshape(occ_dev * vir_dev, aux_width)
    energies = []
    slices = []
    for offset in offsets:
        if offset == 0:
            slices.append(orbitals)
            energies.append(eps_occ)
        else:
            shifted, shifted_energy = shifted_2((orbitals, eps_occ), "occ", -offset)
            slices.append(shifted)
            energies.append(shifted_energy)
    stacked = jnp.stack([one_slice[:, :BATCH_DEV, :] for one_slice in slices])
    row_sets, batch_energy = (
        lax.all_gather(stacked, "vir", axis=2, tiled=True),
        lax.all_gather(eps_vir[:BATCH_DEV], "vir", axis=0, tiled=True),
    )
    batch_width = row_sets.shape[2]
    coulomb = jnp.einsum(
        "rp,cp->rc",
        resident,
        row_sets.reshape(block_count * occ_dev * batch_width, aux_width),
        preferred_element_type=jnp.float32,
    )
    coulomb = coulomb.reshape(occ_dev, vir_dev, block_count, occ_dev, batch_width)
    exchange = jnp.einsum(
        "kjap,ibp->iakjb", jnp.stack(slices), row_sets[REACH], preferred_element_type=jnp.float32
    )
    denominator = pair_energies(eps_occ, jnp.stack(energies), eps_vir, batch_energy)
    amplitude = ((2.0 * coulomb - exchange) / denominator).astype(jnp.bfloat16)
    density = jnp.dot(
        amplitude.reshape(occ_dev * vir_dev, block_count * occ_dev * batch_width),
        row_sets.reshape(block_count * occ_dev * batch_width, aux_width),
        preferred_element_type=jnp.float32,
    )
    return density.reshape(occ_dev, vir_dev, aux_width).astype(jnp.bfloat16)


def solution(mesh):
    return jax.shard_map(
        shards,
        mesh=mesh,
        in_specs=(P("occ", "vir", None), P("occ"), P("vir")),
        out_specs=P("occ", "vir", None),
        check_vma=False,
    )
```

profile of v0, /device:TPU:8, one launch (start us, length us, event | category | flops | bytes accessed | tf_op | source)
XLA Modules:
  0.0 225.0 jit_solution(18331232845301097830)
XLA Ops:
  6.5 1.9 collective-permute-start.1
  8.5 2.4 %collective-permute-start = (bf16[1,256,4096]{2,1,0:T(8,128)(2,1)}, bf16[1,256,4096]{2,1,0:T(8,128)(2,1)S(1)}, u32[]{:S(2)}, u32[]{:S(2)}) collective-permute-start(bf16[1,256,4096]{2,1,0:T(8,128)(2,1)} %param.3), channel_id=1, source_target_pairs={{480,0},{0,32},{32,64},{64,96},{96,128},{128,160},{160,192},{192,2... | collective-permute-start | bytes 6291464 | tf_op jit(solution)/shard_map/ppermute | solution.py:13
  10.9 0.8 slice_bitcast_fusion.12
  11.7 20.6 %collective-permute-done.1 = bf16[1,256,4096]{2,1,0:T(8,128)(2,1)S(1)} collective-permute-done((bf16[1,256,4096]{2,1,0:T(8,128)(2,1)}, bf16[1,256,4096]{2,1,0:T(8,128)(2,1)S(1)}, u32[]{:S(2)}, u32[]{:S(2)}) %collective-permute-start.1) | collective-permute-done | bytes 2097184 | tf_op jit(solution)/shard_map/ppermute | solution.py:13
  32.3 7.9 %collective-permute-done = bf16[1,256,4096]{2,1,0:T(8,128)(2,1)S(1)} collective-permute-done((bf16[1,256,4096]{2,1,0:T(8,128)(2,1)}, bf16[1,256,4096]{2,1,0:T(8,128)(2,1)S(1)}, u32[]{:S(2)}, u32[]{:S(2)}) %collective-permute-start) | collective-permute-done | bytes 2097184 | tf_op jit(solution)/shard_map/ppermute | solution.py:13
  40.2 1.3 copy-done.2
  41.5 0.7 pad_maximum_fusion
  42.2 0.0 all-gather.2.cloned.1.call-update
  42.2 1.9 collective-permute-start.2
  44.2 3.6 %collective-permute-start.3 = (bf16[1]{0:T(256)(128)(2,1)}, bf16[1]{0:T(256)(128)(2,1)}, u32[]{:S(2)}, u32[]{:S(2)}) collective-permute-start(bf16[1]{0:T(256)(128)(2,1)} %param.4), channel_id=1, source_target_pairs={{32,0},{64,32},{96,64},{128,96},{160,128},{192,160},{224,192},{256... | collective-permute-start | bytes 14 | tf_op jit(solution)/shard_map/ppermute | solution.py:13
  48.5 0.7 convert_element_type.25
  49.2 1.3 dynamic-slice
  51.2 0.9 dynamic-update-slice
  52.1 67.1 %all-reduce = bf16[256]{0:T(256)(128)(2,1)S(1)} all-reduce(bf16[256]{0:T(256)(128)(2,1)S(1)} %dynamic-update-slice), channel_id=1, replica_groups=mesh['occ'=16,'vir'=32] {'vir'}, use_global_device_ids=true, to_apply=%add | all-reduce | flops 256 | bytes 1024
  119.1 0.1 add_subtract_fusion
  119.3 0.0 collective-permute-done.2
  119.3 0.0 collective-permute-done.3
  119.3 1.4 maximum_convert_fusion
  120.7 86.0 %all-gather.2.cloned.1.call-done = bf16[3,1,256,4096]{3,2,1,0:T(8,128)(2,1)} async-done(((bf16[3,1,8,4096]{3,2,1,0:T(8,128)(2,1)}), bf16[3,1,256,4096]{3,2,1,0:T(8,128)(2,1)}) %all-gather.2.cloned.1.call-update) | async-done | bytes 6291472 | tf_op jit(solution)/shard_map/all_gather | solution.py:46
  206.7 5.4 %fusion.9 = f32[768,256]{1,0:T(8,128)S(1)} fusion(bf16[768,4096]{1,0:T(8,128)(2,1)} %bitcast.65, bf16[1,256,4096]{2,1,0:T(8,128)(2,1)} %param.3), kind=kOutput, calls=%fused_computation.12 | convolution fusion | flops 1610809344 | bytes 9175040 | tf_op jit(solution)/shard_map/rp,cp->rc/dot_general | solution.py:50
  212.1 0.4 copy-done.1
  212.5 0.6 copy-done.3
  213.1 1.9 fusion.14
  214.9 3.2 %fusion.5 = bf16[1,256,4096]{2,1,0:T(8,128)(2,1)} fusion(bf16[256,768]{0,1:T(8,128)(2,1)S(1)} %bitcast.67, bf16[768,4096]{1,0:T(8,128)(2,1)S(1)} %bitcast.66), kind=kOutput, calls=%fused_computation.7 | convolution fusion | flops 1611661312 | bytes 8781824 | tf_op jit(solution)/shard_map/dot_general | solution.py:62
  (10 shorter events, 0.0 us)
Async XLA Ops:
  6.5 200.1 %all-gather.2.cloned.1.call-start = ((), (), s32[]{:S(2)}) async-start(), calls=%async_computation | async-start | bytes 6488064 | tf_op jit(solution)/shard_map/all_gather | solution.py:46
  6.5 25.8 %collective-permute-start.1 = (bf16[1,256,4096]{2,1,0:T(8,128)(2,1)}, bf16[1,256,4096]{2,1,0:T(8,128)(2,1)S(1)}, u32[]{:S(2)}, u32[]{:S(2)}) collective-permute-start(bf16[1,256,4096]{2,1,0:T(8,128)(2,1)} %param.3), channel_id=1, source_target_pairs={{32,0},{64,32},{96,64},{128,96},{160,128},{192,160},{224,192},{256... | collective-permute-start | bytes 6291464 | tf_op jit(solution)/shard_map/ppermute | solution.py:13
  8.5 31.7 %collective-permute-start = (bf16[1,256,4096]{2,1,0:T(8,128)(2,1)}, bf16[1,256,4096]{2,1,0:T(8,128)(2,1)S(1)}, u32[]{:S(2)}, u32[]{:S(2)}) collective-permute-start(bf16[1,256,4096]{2,1,0:T(8,128)(2,1)} %param.3), channel_id=1, source_target_pairs={{480,0},{0,32},{32,64},{64,96},{96,128},{128,160},{160,192},{192,2... | collective-permute-start | bytes 6291464 | tf_op jit(solution)/shard_map/ppermute | solution.py:13
  40.2 1.3 copy-start.2
  42.2 77.0 %collective-permute-start.2 = (bf16[1]{0:T(256)(128)(2,1)}, bf16[1]{0:T(256)(128)(2,1)}, u32[]{:S(2)}, u32[]{:S(2)}) collective-permute-start(bf16[1]{0:T(256)(128)(2,1)} %param.4), channel_id=1, source_target_pairs={{480,0},{0,32},{32,64},{64,96},{96,128},{128,160},{160,192},{192,2... | collective-permute-start | bytes 14 | tf_op jit(solution)/shard_map/ppermute | solution.py:13
  44.2 75.1 %collective-permute-start.3 = (bf16[1]{0:T(256)(128)(2,1)}, bf16[1]{0:T(256)(128)(2,1)}, u32[]{:S(2)}, u32[]{:S(2)}) collective-permute-start(bf16[1]{0:T(256)(128)(2,1)} %param.4), channel_id=1, source_target_pairs={{32,0},{64,32},{96,64},{128,96},{160,128},{192,160},{224,192},{256... | collective-permute-start | bytes 14 | tf_op jit(solution)/shard_map/ppermute | solution.py:13
  206.6 5.4 %copy-start = (bf16[3,1,256,4096]{3,2,1,0:T(8,128)(2,1)S(1)}, bf16[3,1,256,4096]{3,2,1,0:T(8,128)(2,1)}, u32[]{:S(2)}) copy-start(bf16[3,1,256,4096]{3,2,1,0:T(8,128)(2,1)} %all-gather.2.cloned.1.call-done) | copy-start | bytes 18874372
  206.7 5.8 %copy-start.1 = (bf16[1,256,4096]{2,1,0:T(8,128)(2,1)S(1)}, bf16[1,256,4096]{2,1,0:T(8,128)(2,1)}, u32[]{:S(2)}) copy-start(bf16[1,256,4096]{2,1,0:T(8,128)(2,1)} %param.3) | copy-start | bytes 6291460
  206.7 6.4 %copy-start.3 = (bf16[1,256,4096]{2,1,0:T(8,128)(2,1)S(1)}, bf16[1,256,4096]{2,1,0:T(8,128)(2,1)}, u32[]{:S(2)}) copy-start(bf16[1,256,4096]{2,1,0:T(8,128)(2,1)} %copy-done.2) | copy-start | bytes 6291460
Sparse Core Ops, SparseCore 0:
  42.4 164.2 all-gather.1
where the time goes:
time: 225 us
  waiting for transfers between devices  114 us (51%)
  blocking collectives  67.1 us (30%)
  between operations  14.9 us (7%)
  matrix products  10.5 us (5%)
  starting transfers between devices  9.89 us (4%)
  local copies, waits for them, and re-layouts  5.4 us (2%)
  other arithmetic  2.84 us (1%)
    all_gather x1, waiting for transfers between devices, shards(): lax.all_gather(stacked, 'vir', axis=2, tiled=True)  86 us
    unnamed x1, blocking collectives  67.1 us
    ppermute x4, waiting for transfers between devices, shifted_2(): return lax.ppermute(block, axis, route)  28.5 us
    ppermute x4, starting transfers between devices, shifted_2(): return lax.ppermute(block, axis, route)  9.89 us
    dot_general x1, matrix products, shards(): jnp.einsum('rp,cp->rc', resident, row_sets.reshape(block_count * occ_dev...  5.38 us
    unnamed x11, local copies, waits for them, and re-layouts  4.54 us
  transfers between devices with their start and end apart: 5, of which 3 were waited for; matrix products, arithmetic and copies ran while one was open for 2% of the time, Pallas kernels for 0%

commit v1 on v0

v1 whole, which is shorter than its diff:
```python
import jax
import jax.numpy as jnp
from jax import lax
from jax.experimental import pallas as pl
from jax.experimental.pallas import tpu as pltpu
from jax.sharding import Mesh
from jax.sharding import PartitionSpec as P


BATCH_DEV = 8
CHUNKS = 8
EXTRA = 128

OCC = ("xh", "y", "core")
VIR = ("zq", "zl", "xl")
Z = ("zq", "zl")


def rotate(block, distance):
    size = lax.axis_size(Z)
    return lax.ppermute(block, Z, [((i + distance) % size, i) for i in range(size)])


def pair_up(block):
    size = lax.axis_size(Z)
    return lax.ppermute(block, Z, [((i + 1 if i % 2 else i - 1) % size, i) for i in range(size)])


def swap(block, axis):
    return lax.ppermute(block, axis, [(0, 1), (1, 0)])


def outward(block):
    size = lax.axis_size(OCC)
    route = [((i - 1 if i % 2 == 0 else i + 1) % size, i) for i in range(size)]
    return lax.ppermute(block, OCC, route)


def rows(*blocks):
    return jnp.concatenate(blocks, axis=0)


def contract(a, b):
    return lax.dot_general(a, b, (((1,), (1,)), ((), ())), preferred_element_type=jnp.float32)


def gather_rows(pieces, target, sems, start=0):
    copies, at = [], start
    for n, piece in enumerate(pieces):
        height, width = piece.shape[0], target.shape[1]
        copy = pltpu.make_async_copy(piece.at[:, pl.ds(0, width)], target.at[pl.ds(at, height), :], sems.at[n])
        copy.start()
        copies.append(copy)
        at += height
    return copies


def finish(copies):
    for copy in copies:
        copy.wait()


def own_kernel(vir_ref, x_own, x_mate, x_out, g1, g2, base_ref, a_own_ref, e_mate_ref, e_out_ref, xs, own, tails, sems):
    width = own.shape[1]
    pieces = gather_rows((g1, g2), own, sems)
    for n, (piece, at) in enumerate(((g1, 0), (g2, g1.shape[0]))):
        copy = pltpu.make_async_copy(
            piece.at[:, pl.ds(width, EXTRA)], tails.at[pl.ds(at, piece.shape[0]), :], sems.at[2 + n]
        )
        copy.start()
        pieces.append(copy)
    blocks = [pltpu.make_async_copy(x, xs.at[n], sems.at[4 + n]) for n, x in enumerate((x_own, x_mate, x_out))]
    for copy in blocks:
        copy.start()
    finish(pieces)
    lane = lax.broadcasted_iota(jnp.int32, tails.shape, 1)
    row = lax.broadcasted_iota(jnp.int32, tails.shape, 0)
    tail = tails[...].astype(jnp.float32)
    picked = jnp.where(lane == row % BATCH_DEV, tail, 0.0).astype(jnp.bfloat16)
    batch = contract(jnp.ones((8, EXTRA), jnp.bfloat16), picked)[0:1]
    size = vir_ref.shape[1]
    across = lax.broadcasted_iota(jnp.int32, (size, size), 1) == lax.broadcasted_iota(jnp.int32, (size, size), 0)
    virt = jnp.sum(jnp.where(across, vir_ref[...], 0.0), axis=1, keepdims=True)
    energy = tail[0:1, BATCH_DEV : BATCH_DEV + 1]
    base = virt + batch - energy
    base_ref[...] = base
    blocks[0].wait()
    a_own_ref[...] = (contract(xs[0], own[...]) / (base - energy)).astype(jnp.bfloat16)
    blocks[1].wait()
    e_mate_ref[...] = contract(xs[1], own[...])
    blocks[2].wait()
    e_out_ref[...] = contract(xs[2], own[...])


def pair_amplitude(x_own, block, exchange, base, energy):
    return ((2.0 * contract(x_own, block) - exchange) / (base - energy)).astype(jnp.bfloat16)


def mate_kernel(base_ref, e_mate_ref, tail_ref, x_own, c1, c2, a_mate_ref, xs, mate, sems):
    copies = gather_rows((c1, c2), mate, sems)
    block = pltpu.make_async_copy(x_own, xs, sems.at[2])
    block.start()
    finish(copies)
    block.wait()
    energy = tail_ref[0:1, BATCH_DEV : BATCH_DEV + 1].astype(jnp.float32)
    a_mate_ref[...] = pair_amplitude(xs[...], mate[...], e_mate_ref[...], base_ref[...], energy)


def density_kernel(
    base_ref, e_out_ref, tail_ref, a_own_ref, a_mate_ref, x_own, g1, g2, c1, c2, y1, y2, y3, out_ref, xs, rs, ds, sems
):
    size = base_ref.shape[0]
    out_copies = gather_rows((y1, y2, y3), rs, sems, 2 * size)
    block = pltpu.make_async_copy(x_own, xs, sems.at[3])
    block.start()
    others = gather_rows((g1, g2, c1, c2), rs, sems.at[pl.ds(4, 4)])
    finish(out_copies)
    block.wait()
    energy = tail_ref[0:1, BATCH_DEV : BATCH_DEV + 1].astype(jnp.float32)
    a_out = pair_amplitude(xs[...], rs[pl.ds(2 * size, size), :], e_out_ref[...], base_ref[...], energy)
    finish(others)
    amplitude = jnp.concatenate([a_own_ref[...], a_mate_ref[...], a_out], axis=1)
    stores = []
    for n in range(CHUNKS):
        width = xs.shape[1] // CHUNKS
        at = pl.ds(n * width, width)
        ds[:, at] = jnp.dot(amplitude, rs[:, at], preferred_element_type=jnp.float32).astype(jnp.bfloat16)
        store = pltpu.make_async_copy(ds.at[:, at], out_ref.at[:, at], sems.at[8 + n])
        store.start()
        stores.append(store)
    finish(stores)


def small():
    return pl.BlockSpec(memory_space=pltpu.VMEM)


def large():
    return pl.BlockSpec(memory_space=pl.ANY)


def shards(orbitals, eps_occ, eps_vir):
    x_own = orbitals[0]
    vir_dev, aux = x_own.shape
    x_out = outward(x_own)
    tail = jnp.concatenate([eps_vir[:BATCH_DEV], eps_occ, jnp.zeros(EXTRA - BATCH_DEV - 1, eps_vir.dtype)])
    slab = jnp.concatenate([x_own[:BATCH_DEV], jnp.broadcast_to(tail, (BATCH_DEV, EXTRA))], axis=1)
    n0 = lax.all_gather(slab, "zq", axis=0, tiled=True)
    n0x = swap(n0, "xl")
    up, down = rotate(n0, 1), rotate(n0, -1)
    x_mate = swap(x_own, "core")
    n1 = rows(up, down)
    n1x = swap(n1, "xl")
    even = lax.axis_index("zl") % 2 == 0
    n2 = pair_up(jnp.where(even, up, down))
    g1 = rows(n0, n1, n0x)
    y1 = outward(g1)
    n2x = swap(n2, "xl")
    y2 = outward(rows(n2, n1x))
    g2 = rows(n2, n1x, n2x)
    c1 = swap(g1, "core")
    c2 = swap(g2, "core")
    y3 = outward(n2x)

    batch = g1.shape[0] + g2.shape[0]
    pair_shape = (vir_dev, batch)
    wide = pltpu.VMEM((batch, aux), jnp.bfloat16)
    params = pltpu.CompilerParams(vmem_limit_bytes=24 << 20)
    base, a_own, e_mate, e_out = pl.pallas_call(
        own_kernel,
        out_shape=(
            jax.ShapeDtypeStruct(pair_shape, jnp.float32),
            jax.ShapeDtypeStruct(pair_shape, jnp.bfloat16),
            jax.ShapeDtypeStruct(pair_shape, jnp.float32),
            jax.ShapeDtypeStruct(pair_shape, jnp.float32),
        ),
        in_specs=[small()] + [large()] * 5,
        out_specs=(small(),) * 4,
        scratch_shapes=[
            pltpu.VMEM((3, vir_dev, aux), jnp.bfloat16),
            wide,
            pltpu.VMEM((batch, EXTRA), jnp.bfloat16),
            pltpu.SemaphoreType.DMA((7,)),
        ],
        compiler_params=params,
    )(eps_vir.astype(jnp.float32)[None], x_own, x_mate, x_out, g1, g2)
    a_mate = pl.pallas_call(
        mate_kernel,
        out_shape=jax.ShapeDtypeStruct(pair_shape, jnp.bfloat16),
        in_specs=[small()] * 3 + [large()] * 3,
        out_specs=small(),
        scratch_shapes=[pltpu.VMEM((vir_dev, aux), jnp.bfloat16), wide, pltpu.SemaphoreType.DMA((3,))],
        compiler_params=params,
    )(base, e_mate, c1[:BATCH_DEV, aux:], x_own, c1, c2)
    density = pl.pallas_call(
        density_kernel,
        out_shape=jax.ShapeDtypeStruct((vir_dev, aux), jnp.bfloat16),
        in_specs=[small()] * 5 + [large()] * 8,
        out_specs=large(),
        scratch_shapes=[
            pltpu.VMEM((vir_dev, aux), jnp.bfloat16),
            pltpu.VMEM((3 * batch, aux), jnp.bfloat16),
            pltpu.VMEM((vir_dev, aux), jnp.bfloat16),
            pltpu.SemaphoreType.DMA((8 + CHUNKS,)),
        ],
        compiler_params=params,
    )(base, e_out, y1[:BATCH_DEV, aux:], a_own, a_mate, x_own, g1, g2, c1, c2, y1, y2, y3)
    return density[None]


def solution(mesh):
    fine = Mesh(mesh.devices.reshape(2, 4, 2, 4, 4, 2), OCC + VIR)

    return jax.shard_map(
        shards,
        mesh=fine,
        in_specs=(P(OCC, VIR, None), P(OCC), P(VIR)),
        out_specs=P(OCC, VIR, None),
        check_vma=False,
    )
```

time: 225 us -> 124 us (0.55)
  the two profiles are of different devices: /device:TPU:8 before, /device:TPU:29 now
where the time goes in v1:
time: 124 us
  starting transfers between devices  56.5 us (46%)
  waiting for transfers between devices  30.1 us (24%)
  blocking collectives  20 us (16%)
  Pallas kernels  10.2 us (8%)
  local copies, waits for them, and re-layouts  2.96 us (2%)
  other arithmetic  2.83 us (2%)
    ppermute x4, starting transfers between devices, outward(): return lax.ppermute(block, OCC, route)  28.7 us
    all_gather x1, blocking collectives, shards(): n0 = lax.all_gather(slab, 'zq', axis=0, tiled=True)  20 us
    ppermute x6, starting transfers between devices, swap(): return lax.ppermute(block, axis, [(0, 1), (1, 0)])  18 us
    ppermute x6, waiting for transfers between devices, swap(): return lax.ppermute(block, axis, [(0, 1), (1, 0)])  16.7 us
    ppermute x4, waiting for transfers between devices, outward(): return lax.ppermute(block, OCC, route)  5.74 us
    ppermute x2, starting transfers between devices, rotate(): lax.ppermute(block, Z, [((i + distance) % size, i) for i in range(size)])  5.36 us
    pallas_call x1, Pallas kernels, shards(): pl.pallas_call(density_kernel, out_shape=jax.ShapeDtypeStruct((vir_dev, a...  5.18 us
    ppermute x1, waiting for transfers between devices, pair_up(): lax.ppermute(block, Z, [((i + 1 if i % 2 else i - 1) % size, i) for i in...  5.11 us
  transfers between devices with their start and end apart: 13, of which 5 were waited for; matrix products, arithmetic and copies ran while one was open for 5% of the time, Pallas kernels for 4%

profile of v1, /device:TPU:29, one launch (start us, length us, event | category | flops | bytes accessed | tf_op | source)
XLA Modules:
  0.0 123.5 jit_solution(7080133938121483804)
XLA Ops:
  0.0 2.6 %collective-permute-start = (bf16[256,4096]{1,0:T(8,128)(2,1)}, bf16[256,4096]{1,0:T(8,128)(2,1)S(1)}, u32[]{:S(2)}, u32[]{:S(2)}) collective-permute-start(bf16[256,4096]{1,0:T(8,128)(2,1)} %bitcast.6), channel_id=1, source_target_pairs={{0,32},{32,0},{1,33},{33,1},{2,34},{34,2},{3,35},{35,3},{4,36},{36... | collective-permute-start | bytes 6291464 | tf_op jit(solution)/shard_map/ppermute | solution.py:30
  2.6 7.0 %collective-permute-start.1 = (bf16[256,4096]{1,0:T(8,128)(2,1)}, bf16[256,4096]{1,0:T(8,128)(2,1)}, u32[]{:S(2)}, u32[]{:S(2)}) collective-permute-start(bf16[256,4096]{1,0:T(8,128)(2,1)} %bitcast.7), channel_id=1, source_target_pairs={{480,0},{64,32},{32,64},{128,96},{96,128},{192,160},{160,192},{256... | collective-permute-start | bytes 6291464 | tf_op jit(solution)/shard_map/ppermute | solution.py:36
  11.9 20.0 %all_gather.3 = bf16[32,4224]{1,0:T(8,128)(2,1)} all-gather(bf16[8,4224]{1,0:T(8,128)(2,1)S(1)} %pad_maximum_fusion.2), channel_id=1, replica_groups=mesh['xh'=2,'y'=4,'core'=2,'zq'=4,'zl'=4,'xl'=2] {'zq'}, dimensions={0}, use_global_device_ids=true | all-gather | bytes 337920 | tf_op jit(solution)/shard_map/all_gather | solution.py:148
  31.9 3.4 %collective-permute-start.2 = (bf16[32,4224]{1,0:T(8,128)(2,1)}, bf16[32,4224]{1,0:T(8,128)(2,1)S(1)}, u32[]{:S(2)}, u32[]{:S(2)}) collective-permute-start(bf16[32,4224]{1,0:T(8,128)(2,1)} %all_gather.3), channel_id=1, source_target_pairs={{2,0},{4,2},{6,4},{8,6},{10,8},{12,10},{14,12},{16,14},{18,16},{20... | collective-permute-start | bytes 811016 | tf_op jit(solution)/shard_map/ppermute | solution.py:21
  35.3 1.9 %collective-permute-start.3 = (bf16[32,4224]{1,0:T(8,128)(2,1)}, bf16[32,4224]{1,0:T(8,128)(2,1)}, u32[]{:S(2)}, u32[]{:S(2)}) collective-permute-start(bf16[32,4224]{1,0:T(8,128)(2,1)} %all_gather.3), channel_id=1, source_target_pairs={{30,0},{0,2},{2,4},{4,6},{6,8},{8,10},{10,12},{12,14},{14,16},{16,... | collective-permute-start | bytes 811016 | tf_op jit(solution)/shard_map/ppermute | solution.py:21
  37.3 3.3 %collective-permute-start.4 = (bf16[32,4224]{1,0:T(8,128)(2,1)}, bf16[32,4224]{1,0:T(8,128)(2,1)}, u32[]{:S(2)}, u32[]{:S(2)}) collective-permute-start(bf16[32,4224]{1,0:T(8,128)(2,1)} %all_gather.3), channel_id=1, source_target_pairs={{0,1},{1,0},{2,3},{3,2},{4,5},{5,4},{6,7},{7,6},{8,9},{9,8},{10,11... | collective-permute-start | bytes 811016 | tf_op jit(solution)/shard_map/ppermute | solution.py:30
  41.6 2.5 %collective-permute-done.3 = bf16[32,4224]{1,0:T(8,128)(2,1)} collective-permute-done((bf16[32,4224]{1,0:T(8,128)(2,1)}, bf16[32,4224]{1,0:T(8,128)(2,1)}, u32[]{:S(2)}, u32[]{:S(2)}) %collective-permute-start.3) | collective-permute-done | bytes 270368 | tf_op jit(solution)/shard_map/ppermute | solution.py:21
  44.1 1.0 broadcast_select_fusion
  46.1 12.5 %collective-permute-start.8 = (bf16[128,4224]{1,0:T(8,128)(2,1)S(1)}, bf16[128,4224]{1,0:T(8,128)(2,1)S(1)}, u32[]{:S(2)}, u32[]{:S(2)}) collective-permute-start(bf16[128,4224]{1,0:T(8,128)(2,1)S(1)} %constant_dynamic-update-slice_fusion.g1), channel_id=1, source_target_pairs={{480,0},{64,32},{32,64},{128,96},{96,128},{192,160},{160,192},{256... | collective-permute-start | bytes 3244040 | tf_op jit(solution)/shard_map/ppermute | solution.py:36
  58.5 1.9 %collective-permute-start.9 = (bf16[128,4224]{1,0:T(8,128)(2,1)S(1)}, bf16[128,4224]{1,0:T(8,128)(2,1)S(1)}, u32[]{:S(2)}, u32[]{:S(2)}) collective-permute-start(bf16[128,4224]{1,0:T(8,128)(2,1)S(1)} %constant_dynamic-update-slice_fusion.g1), channel_id=1, source_target_pairs={{0,32},{32,0},{1,33},{33,1},{2,34},{34,2},{3,35},{35,3},{4,36},{36... | collective-permute-start | bytes 3244040 | tf_op jit(solution)/shard_map/ppermute | solution.py:30
  60.5 4.5 %collective-permute-start.5 = (bf16[32,4224]{1,0:T(8,128)(2,1)S(1)}, bf16[32,4224]{1,0:T(8,128)(2,1)S(1)}, u32[]{:S(2)}, u32[]{:S(2)}) collective-permute-start(bf16[32,4224]{1,0:T(8,128)(2,1)S(1)} %get-tuple-element.13), channel_id=1, source_target_pairs={{30,0},{4,2},{2,4},{8,6},{6,8},{12,10},{10,12},{16,14},{14,16},{20... | collective-permute-start | bytes 811016 | tf_op jit(solution)/shard_map/ppermute | solution.py:26
  65.0 1.0 pad_maximum_fusion.1
  66.0 5.1 %collective-permute-done.5 = bf16[32,4224]{1,0:T(8,128)(2,1)S(1)} collective-permute-done((bf16[32,4224]{1,0:T(8,128)(2,1)S(1)}, bf16[32,4224]{1,0:T(8,128)(2,1)S(1)}, u32[]{:S(2)}, u32[]{:S(2)}) %collective-permute-start.5) | collective-permute-done | bytes 270368 | tf_op jit(solution)/shard_map/ppermute | solution.py:26
  71.1 2.6 %collective-permute-start.6 = (bf16[64,4224]{1,0:T(8,128)(2,1)S(1)}, bf16[64,4224]{1,0:T(8,128)(2,1)S(1)}, u32[]{:S(2)}, u32[]{:S(2)}) collective-permute-start(bf16[64,4224]{1,0:T(8,128)(2,1)S(1)} %pad_maximum_fusion.1), channel_id=1, source_target_pairs={{0,1},{1,0},{2,3},{3,2},{4,5},{5,4},{6,7},{7,6},{8,9},{9,8},{10,11... | collective-permute-start | bytes 1622024 | tf_op jit(solution)/shard_map/ppermute | solution.py:30
  73.8 11.7 %collective-permute-done.6 = bf16[64,4224]{1,0:T(8,128)(2,1)S(1)} collective-permute-done((bf16[64,4224]{1,0:T(8,128)(2,1)S(1)}, bf16[64,4224]{1,0:T(8,128)(2,1)S(1)}, u32[]{:S(2)}, u32[]{:S(2)}) %collective-permute-start.6) | collective-permute-done | bytes 540704 | tf_op jit(solution)/shard_map/ppermute | solution.py:30
  85.5 2.6 %collective-permute-start.7 = (bf16[32,4224]{1,0:T(8,128)(2,1)S(1)}, bf16[32,4224]{1,0:T(8,128)(2,1)S(1)}, u32[]{:S(2)}, u32[]{:S(2)}) collective-permute-start(bf16[32,4224]{1,0:T(8,128)(2,1)S(1)} %collective-permute-done.5), channel_id=1, source_target_pairs={{0,1},{1,0},{2,3},{3,2},{4,5},{5,4},{6,7},{7,6},{8,9},{9,8},{10,11... | collective-permute-start | bytes 811016 | tf_op jit(solution)/shard_map/ppermute | solution.py:30
  88.2 5.0 %collective-permute-done.7 = bf16[32,4224]{1,0:T(8,128)(2,1)S(1)} collective-permute-done((bf16[32,4224]{1,0:T(8,128)(2,1)S(1)}, bf16[32,4224]{1,0:T(8,128)(2,1)S(1)}, u32[]{:S(2)}, u32[]{:S(2)}) %collective-permute-start.7) | collective-permute-done | bytes 270368 | tf_op jit(solution)/shard_map/ppermute | solution.py:30
  93.2 5.0 %collective-permute-start.10 = (bf16[128,4224]{1,0:T(8,128)(2,1)S(1)}, bf16[128,4224]{1,0:T(8,128)(2,1)S(1)}, u32[]{:S(2)}, u32[]{:S(2)}) collective-permute-start(bf16[128,4224]{1,0:T(8,128)(2,1)S(1)} %constant_dynamic-update-slice_fusion.4.g2), channel_id=1, source_target_pairs={{0,32},{32,0},{1,33},{33,1},{2,34},{34,2},{3,35},{35,3},{4,36},{36... | collective-permute-start | bytes 3244040 | tf_op jit(solution)/shard_map/ppermute | solution.py:30
  98.3 2.9 %collective-permute-start.11 = (bf16[96,4224]{1,0:T(8,128)(2,1)S(1)}, bf16[96,4224]{1,0:T(8,128)(2,1)S(1)}, u32[]{:S(2)}, u32[]{:S(2)}) collective-permute-start(bf16[96,4224]{1,0:T(8,128)(2,1)S(1)} %pad_maximum_fusion), channel_id=1, source_target_pairs={{480,0},{64,32},{32,64},{128,96},{96,128},{192,160},{160,192},{256... | collective-permute-start | bytes 2433032 | tf_op jit(solution)/shard_map/ppermute | solution.py:36
  101.2 6.3 %collective-permute-start.12 = (bf16[32,4224]{1,0:T(8,128)(2,1)S(1)}, bf16[32,4224]{1,0:T(8,128)(2,1)S(1)}, u32[]{:S(2)}, u32[]{:S(2)}) collective-permute-start(bf16[32,4224]{1,0:T(8,128)(2,1)S(1)} %collective-permute-done.7), channel_id=1, source_target_pairs={{480,0},{64,32},{32,64},{128,96},{96,128},{192,160},{160,192},{256... | collective-permute-start | bytes 811016 | tf_op jit(solution)/shard_map/ppermute | solution.py:36
  107.6 4.0 %shard_map.37 = (f32[256,256]{1,0:T(8,128)S(1)}, bf16[256,256]{1,0:T(8,128)(2,1)S(1)}, f32[256,256]{1,0:T(8,128)S(1)}, f32[256,256]{1,0:T(8,128)S(1)}) custom-call(f32[1,256]{1,0:T(1,128)S(1)} %bitcast.11, bf16[256,4096]{1,0:T(8,128)(2,1)S(1)} %bitcast.8, bf16[256,4096]{1,0:T(8,128)(2,1)S(1)} %collective-permute-done.x_mate, ...), custom_call_target="tpu_custom_call" | custom-call | tf_op jit(solution)/shard_map/pallas_call | solution.py:169
  111.6 1.1 shard_map.38.a_mate_ref
  112.6 5.7 %collective-permute-done.12.y3 = bf16[32,4224]{1,0:T(8,128)(2,1)S(1)} collective-permute-done((bf16[32,4224]{1,0:T(8,128)(2,1)S(1)}, bf16[32,4224]{1,0:T(8,128)(2,1)S(1)}, u32[]{:S(2)}, u32[]{:S(2)}) %collective-permute-start.12) | collective-permute-done | bytes 270368 | tf_op jit(solution)/shard_map/ppermute | solution.py:36
  118.4 5.2 %shard_map.39 = bf16[256,4096]{1,0:T(8,128)(2,1)} custom-call(f32[256,256]{1,0:T(8,128)S(1)} %get-tuple-element.9.base_ref, f32[256,256]{1,0:T(8,128)S(1)} %get-tuple-element.10.e_out_ref, bf16[8,128]{1,0:T(8,128)(2,1)S(1)} %slice.20.tail_ref, bf16[256,256]{1,0:T(8,128)(2,1)S(1)} %get-tuple-element.11.a_own_ref, bf16[256,256]{1,0:T(8,128)(2,1)S(1)} %shard_map.38.a_mate_ref, ...), custom_call_target="tpu_custom_call" | custom-call | tf_op jit(solution)/shard_map/pallas_call | solution.py:195
  (26 shorter events, 3.8 us)
Async XLA Ops:
  0.0 107.5 %collective-permute-start = (bf16[256,4096]{1,0:T(8,128)(2,1)}, bf16[256,4096]{1,0:T(8,128)(2,1)S(1)}, u32[]{:S(2)}, u32[]{:S(2)}) collective-permute-start(bf16[256,4096]{1,0:T(8,128)(2,1)} %bitcast.6), channel_id=1, source_target_pairs={{0,32},{32,0},{1,33},{33,1},{2,34},{34,2},{3,35},{35,3},{4,36},{36... | collective-permute-start | bytes 6291464 | tf_op jit(solution)/shard_map/ppermute | solution.py:30
  2.6 105.0 %collective-permute-start.1 = (bf16[256,4096]{1,0:T(8,128)(2,1)}, bf16[256,4096]{1,0:T(8,128)(2,1)}, u32[]{:S(2)}, u32[]{:S(2)}) collective-permute-start(bf16[256,4096]{1,0:T(8,128)(2,1)} %bitcast.7), channel_id=1, source_target_pairs={{480,0},{64,32},{32,64},{128,96},{96,128},{192,160},{160,192},{256... | collective-permute-start | bytes 6291464 | tf_op jit(solution)/shard_map/ppermute | solution.py:36
  31.9 9.7 %collective-permute-start.2 = (bf16[32,4224]{1,0:T(8,128)(2,1)}, bf16[32,4224]{1,0:T(8,128)(2,1)S(1)}, u32[]{:S(2)}, u32[]{:S(2)}) collective-permute-start(bf16[32,4224]{1,0:T(8,128)(2,1)} %all_gather.3), channel_id=1, source_target_pairs={{2,0},{4,2},{6,4},{8,6},{10,8},{12,10},{14,12},{16,14},{18,16},{20... | collective-permute-start | bytes 811016 | tf_op jit(solution)/shard_map/ppermute | solution.py:21
  35.3 8.7 %collective-permute-start.3 = (bf16[32,4224]{1,0:T(8,128)(2,1)}, bf16[32,4224]{1,0:T(8,128)(2,1)}, u32[]{:S(2)}, u32[]{:S(2)}) collective-permute-start(bf16[32,4224]{1,0:T(8,128)(2,1)} %all_gather.3), channel_id=1, source_target_pairs={{30,0},{0,2},{2,4},{4,6},{6,8},{8,10},{10,12},{12,14},{14,16},{16,... | collective-permute-start | bytes 811016 | tf_op jit(solution)/shard_map/ppermute | solution.py:21
  37.3 7.8 %collective-permute-start.4 = (bf16[32,4224]{1,0:T(8,128)(2,1)}, bf16[32,4224]{1,0:T(8,128)(2,1)}, u32[]{:S(2)}, u32[]{:S(2)}) collective-permute-start(bf16[32,4224]{1,0:T(8,128)(2,1)} %all_gather.3), channel_id=1, source_target_pairs={{0,1},{1,0},{2,3},{3,2},{4,5},{5,4},{6,7},{7,6},{8,9},{9,8},{10,11... | collective-permute-start | bytes 811016 | tf_op jit(solution)/shard_map/ppermute | solution.py:30
  46.1 52.2 %collective-permute-start.8 = (bf16[128,4224]{1,0:T(8,128)(2,1)S(1)}, bf16[128,4224]{1,0:T(8,128)(2,1)S(1)}, u32[]{:S(2)}, u32[]{:S(2)}) collective-permute-start(bf16[128,4224]{1,0:T(8,128)(2,1)S(1)} %constant_dynamic-update-slice_fusion.g1), channel_id=1, source_target_pairs={{480,0},{64,32},{32,64},{128,96},{96,128},{192,160},{160,192},{256... | collective-permute-start | bytes 3244040 | tf_op jit(solution)/shard_map/ppermute | solution.py:36
  58.5 42.6 %collective-permute-start.9 = (bf16[128,4224]{1,0:T(8,128)(2,1)S(1)}, bf16[128,4224]{1,0:T(8,128)(2,1)S(1)}, u32[]{:S(2)}, u32[]{:S(2)}) collective-permute-start(bf16[128,4224]{1,0:T(8,128)(2,1)S(1)} %constant_dynamic-update-slice_fusion.g1), channel_id=1, source_target_pairs={{0,32},{32,0},{1,33},{33,1},{2,34},{34,2},{3,35},{35,3},{4,36},{36... | collective-permute-start | bytes 3244040 | tf_op jit(solution)/shard_map/ppermute | solution.py:30
  60.5 10.6 %collective-permute-start.5 = (bf16[32,4224]{1,0:T(8,128)(2,1)S(1)}, bf16[32,4224]{1,0:T(8,128)(2,1)S(1)}, u32[]{:S(2)}, u32[]{:S(2)}) collective-permute-start(bf16[32,4224]{1,0:T(8,128)(2,1)S(1)} %get-tuple-element.13), channel_id=1, source_target_pairs={{30,0},{4,2},{2,4},{8,6},{6,8},{12,10},{10,12},{16,14},{14,16},{20... | collective-permute-start | bytes 811016 | tf_op jit(solution)/shard_map/ppermute | solution.py:26
  71.1 14.4 %collective-permute-start.6 = (bf16[64,4224]{1,0:T(8,128)(2,1)S(1)}, bf16[64,4224]{1,0:T(8,128)(2,1)S(1)}, u32[]{:S(2)}, u32[]{:S(2)}) collective-permute-start(bf16[64,4224]{1,0:T(8,128)(2,1)S(1)} %pad_maximum_fusion.1), channel_id=1, source_target_pairs={{0,1},{1,0},{2,3},{3,2},{4,5},{5,4},{6,7},{7,6},{8,9},{9,8},{10,11... | collective-permute-start | bytes 1622024 | tf_op jit(solution)/shard_map/ppermute | solution.py:30
  85.5 7.7 %collective-permute-start.7 = (bf16[32,4224]{1,0:T(8,128)(2,1)S(1)}, bf16[32,4224]{1,0:T(8,128)(2,1)S(1)}, u32[]{:S(2)}, u32[]{:S(2)}) collective-permute-start(bf16[32,4224]{1,0:T(8,128)(2,1)S(1)} %collective-permute-done.5), channel_id=1, source_target_pairs={{0,1},{1,0},{2,3},{3,2},{4,5},{5,4},{6,7},{7,6},{8,9},{9,8},{10,11... | collective-permute-start | bytes 811016 | tf_op jit(solution)/shard_map/ppermute | solution.py:30
  88.2 19.3 %copy-start.1 = (bf16[256]{0:T(256)(128)(2,1)S(1)}, bf16[256]{0:T(256)(128)(2,1)}, u32[]{:S(2)}) copy-start(bf16[256]{0:T(256)(128)(2,1)} %param.5) | copy-start | bytes 1540
  88.2 19.4 %copy-start = (bf16[1,256,4096]{2,1,0:T(8,128)(2,1)S(1)}, bf16[1,256,4096]{2,1,0:T(8,128)(2,1)}, u32[]{:S(2)}) copy-start(bf16[1,256,4096]{2,1,0:T(8,128)(2,1)} %param.3) | copy-start | bytes 6291460
  93.2 18.3 %collective-permute-start.10 = (bf16[128,4224]{1,0:T(8,128)(2,1)S(1)}, bf16[128,4224]{1,0:T(8,128)(2,1)S(1)}, u32[]{:S(2)}, u32[]{:S(2)}) collective-permute-start(bf16[128,4224]{1,0:T(8,128)(2,1)S(1)} %constant_dynamic-update-slice_fusion.4.g2), channel_id=1, source_target_pairs={{0,32},{32,0},{1,33},{33,1},{2,34},{34,2},{3,35},{35,3},{4,36},{36... | collective-permute-start | bytes 3244040 | tf_op jit(solution)/shard_map/ppermute | solution.py:30
  98.3 20.1 %collective-permute-start.11 = (bf16[96,4224]{1,0:T(8,128)(2,1)S(1)}, bf16[96,4224]{1,0:T(8,128)(2,1)S(1)}, u32[]{:S(2)}, u32[]{:S(2)}) collective-permute-start(bf16[96,4224]{1,0:T(8,128)(2,1)S(1)} %pad_maximum_fusion), channel_id=1, source_target_pairs={{480,0},{64,32},{32,64},{128,96},{96,128},{192,160},{160,192},{256... | collective-permute-start | bytes 2433032 | tf_op jit(solution)/shard_map/ppermute | solution.py:36
  101.2 17.2 %collective-permute-start.12 = (bf16[32,4224]{1,0:T(8,128)(2,1)S(1)}, bf16[32,4224]{1,0:T(8,128)(2,1)S(1)}, u32[]{:S(2)}, u32[]{:S(2)}) collective-permute-start(bf16[32,4224]{1,0:T(8,128)(2,1)S(1)} %collective-permute-done.7), channel_id=1, source_target_pairs={{480,0},{64,32},{32,64},{128,96},{96,128},{192,160},{160,192},{256... | collective-permute-start | bytes 811016 | tf_op jit(solution)/shard_map/ppermute | solution.py:36

commit v2 on v1

--- a/solution.py
+++ b/solution.py
@@ -60,16 +60,18 @@
         copy.wait()
 
 
-def own_kernel(vir_ref, x_own, x_mate, x_out, g1, g2, base_ref, a_own_ref, e_mate_ref, e_out_ref, xs, own, tails, sems):
+def own_kernel(vir_ref, x_own, x_mate, x_out, p1, p2, p3, base_ref, a_own_ref, e_mate_ref, e_out_ref, xs, own, tails, sems):
     width = own.shape[1]
-    pieces = gather_rows((g1, g2), own, sems)
-    for n, (piece, at) in enumerate(((g1, 0), (g2, g1.shape[0]))):
+    pieces = gather_rows((p1, p2, p3), own, sems)
+    at = 0
+    for n, piece in enumerate((p1, p2, p3)):
         copy = pltpu.make_async_copy(
-            piece.at[:, pl.ds(width, EXTRA)], tails.at[pl.ds(at, piece.shape[0]), :], sems.at[2 + n]
+            piece.at[:, pl.ds(width, EXTRA)], tails.at[pl.ds(at, piece.shape[0]), :], sems.at[3 + n]
         )
         copy.start()
         pieces.append(copy)
-    blocks = [pltpu.make_async_copy(x, xs.at[n], sems.at[4 + n]) for n, x in enumerate((x_own, x_mate, x_out))]
+        at += piece.shape[0]
+    blocks = [pltpu.make_async_copy(x, xs.at[n], sems.at[6 + n]) for n, x in enumerate((x_own, x_mate, x_out))]
     for copy in blocks:
         copy.start()
     finish(pieces)
@@ -96,9 +98,9 @@
     return ((2.0 * contract(x_own, block) - exchange) / (base - energy)).astype(jnp.bfloat16)
 
 
-def mate_kernel(base_ref, e_mate_ref, tail_ref, x_own, c1, c2, a_mate_ref, xs, mate, sems):
-    copies = gather_rows((c1, c2), mate, sems)
-    block = pltpu.make_async_copy(x_own, xs, sems.at[2])
+def mate_kernel(base_ref, e_mate_ref, tail_ref, x_own, c1, c2, c3, a_mate_ref, xs, mate, sems):
+    copies = gather_rows((c1, c2, c3), mate, sems)
+    block = pltpu.make_async_copy(x_own, xs, sems.at[3])
     block.start()
     finish(copies)
     block.wait()
@@ -106,14 +108,13 @@
     a_mate_ref[...] = pair_amplitude(xs[...], mate[...], e_mate_ref[...], base_ref[...], energy)
 
 
-def density_kernel(
-    base_ref, e_out_ref, tail_ref, a_own_ref, a_mate_ref, x_own, g1, g2, c1, c2, y1, y2, y3, out_ref, xs, rs, ds, sems
-):
+def density_kernel(base_ref, e_out_ref, tail_ref, a_own_ref, a_mate_ref, x_own, *refs):
+    *pieces, out_ref, xs, rs, ds, sems = refs
     size = base_ref.shape[0]
-    out_copies = gather_rows((y1, y2, y3), rs, sems, 2 * size)
+    out_copies = gather_rows(pieces[6:], rs, sems, 2 * size)
     block = pltpu.make_async_copy(x_own, xs, sems.at[3])
     block.start()
-    others = gather_rows((g1, g2, c1, c2), rs, sems.at[pl.ds(4, 4)])
+    others = gather_rows(pieces[:6], rs, sems.at[pl.ds(4, 6)])
     finish(out_copies)
     block.wait()
     energy = tail_ref[0:1, BATCH_DEV : BATCH_DEV + 1].astype(jnp.float32)
@@ -125,7 +126,7 @@
         width = xs.shape[1] // CHUNKS
         at = pl.ds(n * width, width)
         ds[:, at] = jnp.dot(amplitude, rs[:, at], preferred_element_type=jnp.float32).astype(jnp.bfloat16)
-        store = pltpu.make_async_copy(ds.at[:, at], out_ref.at[:, at], sems.at[8 + n])
+        store = pltpu.make_async_copy(ds.at[:, at], out_ref.at[:, at], sems.at[10 + n])
         store.start()
         stores.append(store)
     finish(stores)
@@ -145,24 +146,22 @@
     x_out = outward(x_own)
     tail = jnp.concatenate([eps_vir[:BATCH_DEV], eps_occ, jnp.zeros(EXTRA - BATCH_DEV - 1, eps_vir.dtype)])
     slab = jnp.concatenate([x_own[:BATCH_DEV], jnp.broadcast_to(tail, (BATCH_DEV, EXTRA))], axis=1)
-    n0 = lax.all_gather(slab, "zq", axis=0, tiled=True)
-    n0x = swap(n0, "xl")
-    up, down = rotate(n0, 1), rotate(n0, -1)
+    part = lax.all_gather(slab, "zq", axis=0, tiled=True)
+    first = rows(part, swap(part, "xl"))
+    up, down = rotate(first, 1), rotate(first, -1)
     x_mate = swap(x_own, "core")
-    n1 = rows(up, down)
-    n1x = swap(n1, "xl")
+    y1 = outward(first)
+    c1 = swap(first, "core")
     even = lax.axis_index("zl") % 2 == 0
-    n2 = pair_up(jnp.where(even, up, down))
-    g1 = rows(n0, n1, n0x)
-    y1 = outward(g1)
-    n2x = swap(n2, "xl")
-    y2 = outward(rows(n2, n1x))
-    g2 = rows(n2, n1x, n2x)
-    c1 = swap(g1, "core")
-    c2 = swap(g2, "core")
-    y3 = outward(n2x)
-
-    batch = g1.shape[0] + g2.shape[0]
+    third = pair_up(jnp.where(even, up, down))
+    second = rows(up, down)
+    y2 = outward(second)
+    c2 = swap(second, "core")
+    y3 = outward(third)
+    c3 = swap(third, "core")
+    own, mate, out = (first, second, third), (c1, c2, c3), (y1, y2, y3)
+
+    batch = sum(piece.shape[0] for piece in own)
     pair_shape = (vir_dev, batch)
     wide = pltpu.VMEM((batch, aux), jnp.bfloat16)
     params = pltpu.CompilerParams(vmem_limit_bytes=24 << 20)
@@ -174,37 +173,37 @@
             jax.ShapeDtypeStruct(pair_shape, jnp.float32),
             jax.ShapeDtypeStruct(pair_shape, jnp.float32),
         ),
-        in_specs=[small()] + [large()] * 5,
+        in_specs=[small()] + [large()] * 6,
         out_specs=(small(),) * 4,
         scratch_shapes=[
             pltpu.VMEM((3, vir_dev, aux), jnp.bfloat16),
             wide,
             pltpu.VMEM((batch, EXTRA), jnp.bfloat16),
-            pltpu.SemaphoreType.DMA((7,)),
+            pltpu.SemaphoreType.DMA((9,)),
         ],
         compiler_params=params,
-    )(eps_vir.astype(jnp.float32)[None], x_own, x_mate, x_out, g1, g2)
+    )(eps_vir.astype(jnp.float32)[None], x_own, x_mate, x_out, *own)
     a_mate = pl.pallas_call(
         mate_kernel,
         out_shape=jax.ShapeDtypeStruct(pair_shape, jnp.bfloat16),
-        in_specs=[small()] * 3 + [large()] * 3,
+        in_specs=[small()] * 3 + [large()] * 4,
         out_specs=small(),
-        scratch_shapes=[pltpu.VMEM((vir_dev, aux), jnp.bfloat16), wide, pltpu.SemaphoreType.DMA((3,))],
+        scratch_shapes=[pltpu.VMEM((vir_dev, aux), jnp.bfloat16), wide, pltpu.SemaphoreType.DMA((4,))],
         compiler_params=params,
-    )(base, e_mate, c1[:BATCH_DEV, aux:], x_own, c1, c2)
+    )(base, e_mate, c1[:BATCH_DEV, aux:], x_own, *mate)
     density = pl.pallas_call(
         density_kernel,
         out_shape=jax.ShapeDtypeStruct((vir_dev, aux), jnp.bfloat16),
-        in_specs=[small()] * 5 + [large()] * 8,
+        in_specs=[small()] * 5 + [large()] * 10,
         out_specs=large(),
         scratch_shapes=[
             pltpu.VMEM((vir_dev, aux), jnp.bfloat16),
             pltpu.VMEM((3 * batch, aux), jnp.bfloat16),
             pltpu.VMEM((vir_dev, aux), jnp.bfloat16),
-            pltpu.SemaphoreType.DMA((8 + CHUNKS,)),
+            pltpu.SemaphoreType.DMA((10 + CHUNKS,)),
         ],
         compiler_params=params,
-    )(base, e_out, y1[:BATCH_DEV, aux:], a_own, a_mate, x_own, g1, g2, c1, c2, y1, y2, y3)
+    )(base, e_out, y1[:BATCH_DEV, aux:], a_own, a_mate, x_own, *own, *mate, *out)
     return density[None]
 
 

time: 124 us -> 113 us (0.911)
  the two profiles are of different devices: /device:TPU:29 before, /device:TPU:27 now
where the time goes in v2:
time: 113 us; the launch traced here: 112 us
  starting transfers between devices  41.1 us (36%)
  waiting for transfers between devices  33.8 us (30%)
  blocking collectives  24.4 us (22%)
  Pallas kernels  10.3 us (9%)
    all_gather x1, blocking collectives, shards(): part = lax.all_gather(slab, 'zq', axis=0, tiled=True)  24.4 us
    ppermute x4, waiting for transfers between devices, outward(): return lax.ppermute(block, OCC, route)  21.5 us
    ppermute x4, starting transfers between devices, outward(): return lax.ppermute(block, OCC, route)  18.6 us
    ppermute x5, starting transfers between devices, swap(): return lax.ppermute(block, axis, [(0, 1), (1, 0)])  14.8 us
    ppermute x2, waiting for transfers between devices, rotate(): lax.ppermute(block, Z, [((i + distance) % size, i) for i in range(size)])  7.19 us
    ppermute x2, starting transfers between devices, rotate(): lax.ppermute(block, Z, [((i + distance) % size, i) for i in range(size)])  5.79 us
    pallas_call x1, Pallas kernels, shards(): pl.pallas_call(density_kernel, out_shape=jax.ShapeDtypeStruct((vir_dev, a...  5.21 us
    ppermute x5, waiting for transfers between devices, swap(): return lax.ppermute(block, axis, [(0, 1), (1, 0)])  5.02 us
  transfers between devices with their start and end apart: 12, of which 4 were waited for; matrix products, arithmetic and copies ran while one was open for 0% of the time, Pallas kernels for 5%

profile of v2, /device:TPU:27, one launch (start us, length us, event | category | flops | bytes accessed | tf_op | source)
XLA Modules:
  0.0 112.4 jit_solution(14150897477537733157)
XLA Ops:
  0.0 0.8 slice_bitcast_fusion
  1.5 0.7 pad_maximum_fusion.1
  2.3 24.4 %all_gather.3 = bf16[32,4224]{1,0:T(8,128)(2,1)S(1)} all-gather(bf16[8,4224]{1,0:T(8,128)(2,1)S(1)} %pad_maximum_fusion), channel_id=1, replica_groups=mesh['xh'=2,'y'=4,'core'=2,'zq'=4,'zl'=4,'xl'=2] {'zq'}, dimensions={0}, use_global_device_ids=true | all-gather | bytes 337920 | tf_op jit(solution)/shard_map/all_gather | solution.py:149
  26.7 2.2 %collective-permute-start.2 = (bf16[32,4224]{1,0:T(8,128)(2,1)S(1)}, bf16[32,4224]{1,0:T(8,128)(2,1)S(1)}, u32[]{:S(2)}, u32[]{:S(2)}) collective-permute-start(bf16[32,4224]{1,0:T(8,128)(2,1)S(1)} %all_gather.3), channel_id=1, source_target_pairs={{0,1},{1,0},{2,3},{3,2},{4,5},{5,4},{6,7},{7,6},{8,9},{9,8},{10,11... | collective-permute-start | bytes 811016 | tf_op jit(solution)/shard_map/ppermute | solution.py:30
  28.9 5.0 %collective-permute-done.2 = bf16[32,4224]{1,0:T(8,128)(2,1)S(1)} collective-permute-done((bf16[32,4224]{1,0:T(8,128)(2,1)S(1)}, bf16[32,4224]{1,0:T(8,128)(2,1)S(1)}, u32[]{:S(2)}, u32[]{:S(2)}) %collective-permute-start.2) | collective-permute-done | bytes 270368 | tf_op jit(solution)/shard_map/ppermute | solution.py:30
  33.9 3.9 %collective-permute-start.3 = (bf16[64,4224]{1,0:T(8,128)(2,1)S(1)}, bf16[64,4224]{1,0:T(8,128)(2,1)S(1)}, u32[]{:S(2)}, u32[]{:S(2)}) collective-permute-start(bf16[64,4224]{1,0:T(8,128)(2,1)S(1)} %constant_dynamic-update-slice_fusion.p1.refs_0_), channel_id=1, source_target_pairs={{2,0},{4,2},{6,4},{8,6},{10,8},{12,10},{14,12},{16,14},{18,16},{20... | collective-permute-start | bytes 1622024 | tf_op jit(solution)/shard_map/ppermute | solution.py:21
  37.8 6.5 %collective-permute-start = (bf16[256,4096]{1,0:T(8,128)(2,1)}, bf16[256,4096]{1,0:T(8,128)(2,1)S(1)}, u32[]{:S(2)}, u32[]{:S(2)}) collective-permute-start(bf16[256,4096]{1,0:T(8,128)(2,1)} %bitcast.6), channel_id=1, source_target_pairs={{0,32},{32,0},{1,33},{33,1},{2,34},{34,2},{3,35},{35,3},{4,36},{36... | collective-permute-start | bytes 6291464 | tf_op jit(solution)/shard_map/ppermute | solution.py:30
  44.3 3.3 %collective-permute-start.1 = (bf16[256,4096]{1,0:T(8,128)(2,1)}, bf16[256,4096]{1,0:T(8,128)(2,1)}, u32[]{:S(2)}, u32[]{:S(2)}) collective-permute-start(bf16[256,4096]{1,0:T(8,128)(2,1)} %bitcast.7), channel_id=1, source_target_pairs={{480,0},{64,32},{32,64},{128,96},{96,128},{192,160},{160,192},{256... | collective-permute-start | bytes 6291464 | tf_op jit(solution)/shard_map/ppermute | solution.py:36
  47.6 1.9 %collective-permute-start.4 = (bf16[64,4224]{1,0:T(8,128)(2,1)S(1)}, bf16[64,4224]{1,0:T(8,128)(2,1)S(1)}, u32[]{:S(2)}, u32[]{:S(2)}) collective-permute-start(bf16[64,4224]{1,0:T(8,128)(2,1)S(1)} %constant_dynamic-update-slice_fusion.p1.refs_0_), channel_id=1, source_target_pairs={{30,0},{0,2},{2,4},{4,6},{6,8},{8,10},{10,12},{12,14},{14,16},{16,... | collective-permute-start | bytes 1622024 | tf_op jit(solution)/shard_map/ppermute | solution.py:21
  49.6 1.9 %collective-permute-start.7 = (bf16[64,4224]{1,0:T(8,128)(2,1)S(1)}, bf16[64,4224]{1,0:T(8,128)(2,1)S(1)}, u32[]{:S(2)}, u32[]{:S(2)}) collective-permute-start(bf16[64,4224]{1,0:T(8,128)(2,1)S(1)} %constant_dynamic-update-slice_fusion.p1.refs_0_), channel_id=1, source_target_pairs={{0,32},{32,0},{1,33},{33,1},{2,34},{34,2},{3,35},{35,3},{4,36},{36... | collective-permute-start | bytes 1622024 | tf_op jit(solution)/shard_map/ppermute | solution.py:30
  51.5 6.1 %collective-permute-start.6 = (bf16[64,4224]{1,0:T(8,128)(2,1)S(1)}, bf16[64,4224]{1,0:T(8,128)(2,1)S(1)}, u32[]{:S(2)}, u32[]{:S(2)}) collective-permute-start(bf16[64,4224]{1,0:T(8,128)(2,1)S(1)} %constant_dynamic-update-slice_fusion.p1.refs_0_), channel_id=1, source_target_pairs={{480,0},{64,32},{32,64},{128,96},{96,128},{192,160},{160,192},{256... | collective-permute-start | bytes 1622024 | tf_op jit(solution)/shard_map/ppermute | solution.py:36
  57.7 0.0 copy-start.1
  57.7 7.2 %collective-permute-done.4 = bf16[64,4224]{1,0:T(8,128)(2,1)S(1)} collective-permute-done((bf16[64,4224]{1,0:T(8,128)(2,1)S(1)}, bf16[64,4224]{1,0:T(8,128)(2,1)S(1)}, u32[]{:S(2)}, u32[]{:S(2)}) %collective-permute-start.4) | collective-permute-done | bytes 540704 | tf_op jit(solution)/shard_map/ppermute | solution.py:21
  64.9 0.2 broadcast_select_fusion
  65.0 1.9 %collective-permute-start.5 = (bf16[64,4224]{1,0:T(8,128)(2,1)S(1)}, bf16[64,4224]{1,0:T(8,128)(2,1)S(1)}, u32[]{:S(2)}, u32[]{:S(2)}) collective-permute-start(bf16[64,4224]{1,0:T(8,128)(2,1)S(1)} %get-tuple-element.13), channel_id=1, source_target_pairs={{30,0},{4,2},{2,4},{8,6},{6,8},{12,10},{10,12},{16,14},{14,16},{20... | collective-permute-start | bytes 1622024 | tf_op jit(solution)/shard_map/ppermute | solution.py:26
  67.0 2.3 %collective-permute-start.8 = (bf16[128,4224]{1,0:T(8,128)(2,1)S(1)}, bf16[128,4224]{1,0:T(8,128)(2,1)S(1)}, u32[]{:S(2)}, u32[]{:S(2)}) collective-permute-start(bf16[128,4224]{1,0:T(8,128)(2,1)S(1)} %get-tuple-element.14.p2.refs_1_), channel_id=1, source_target_pairs={{0,32},{32,0},{1,33},{33,1},{2,34},{34,2},{3,35},{35,3},{4,36},{36... | collective-permute-start | bytes 3244040 | tf_op jit(solution)/shard_map/ppermute | solution.py:30
  69.3 12.0 %collective-permute-done.6.refs_6_ = bf16[64,4224]{1,0:T(8,128)(2,1)S(1)} collective-permute-done((bf16[64,4224]{1,0:T(8,128)(2,1)S(1)}, bf16[64,4224]{1,0:T(8,128)(2,1)S(1)}, u32[]{:S(2)}, u32[]{:S(2)}) %collective-permute-start.6) | collective-permute-done | bytes 540704 | tf_op jit(solution)/shard_map/ppermute | solution.py:36
  81.3 3.3 %collective-permute-start.10 = (bf16[128,4224]{1,0:T(8,128)(2,1)S(1)}, bf16[128,4224]{1,0:T(8,128)(2,1)S(1)}, u32[]{:S(2)}, u32[]{:S(2)}) collective-permute-start(bf16[128,4224]{1,0:T(8,128)(2,1)S(1)} %get-tuple-element.14.p2.refs_1_), channel_id=1, source_target_pairs={{480,0},{64,32},{32,64},{128,96},{96,128},{192,160},{160,192},{256... | collective-permute-start | bytes 3244040 | tf_op jit(solution)/shard_map/ppermute | solution.py:36
  84.6 1.9 %collective-permute-start.9 = (bf16[64,4224]{1,0:T(8,128)(2,1)S(1)}, bf16[64,4224]{1,0:T(8,128)(2,1)S(1)}, u32[]{:S(2)}, u32[]{:S(2)}) collective-permute-start(bf16[64,4224]{1,0:T(8,128)(2,1)S(1)} %collective-permute-done.5.p3.refs_2_), channel_id=1, source_target_pairs={{0,32},{32,0},{1,33},{33,1},{2,34},{34,2},{3,35},{35,3},{4,36},{36... | collective-permute-start | bytes 1622024 | tf_op jit(solution)/shard_map/ppermute | solution.py:30
  86.5 5.9 %collective-permute-start.11 = (bf16[64,4224]{1,0:T(8,128)(2,1)S(1)}, bf16[64,4224]{1,0:T(8,128)(2,1)S(1)}, u32[]{:S(2)}, u32[]{:S(2)}) collective-permute-start(bf16[64,4224]{1,0:T(8,128)(2,1)S(1)} %collective-permute-done.5.p3.refs_2_), channel_id=1, source_target_pairs={{480,0},{64,32},{32,64},{128,96},{96,128},{192,160},{160,192},{256... | collective-permute-start | bytes 1622024 | tf_op jit(solution)/shard_map/ppermute | solution.py:36
  92.5 4.0 %shard_map.37 = (f32[256,256]{1,0:T(8,128)S(1)}, bf16[256,256]{1,0:T(8,128)(2,1)S(1)}, f32[256,256]{1,0:T(8,128)S(1)}, f32[256,256]{1,0:T(8,128)S(1)}) custom-call(f32[1,256]{1,0:T(1,128)S(1)} %bitcast.11, bf16[256,4096]{1,0:T(8,128)(2,1)S(1)} %bitcast.8, bf16[256,4096]{1,0:T(8,128)(2,1)S(1)} %collective-permute-done.x_mate, ...), custom_call_target="tpu_custom_call" | custom-call | tf_op jit(solution)/shard_map/pallas_call | solution.py:168
  96.5 1.1 shard_map.38.a_mate_ref
  97.6 9.5 %collective-permute-done.11.refs_8_ = bf16[64,4224]{1,0:T(8,128)(2,1)S(1)} collective-permute-done((bf16[64,4224]{1,0:T(8,128)(2,1)S(1)}, bf16[64,4224]{1,0:T(8,128)(2,1)S(1)}, u32[]{:S(2)}, u32[]{:S(2)}) %collective-permute-start.11) | collective-permute-done | bytes 540704 | tf_op jit(solution)/shard_map/ppermute | solution.py:36
  107.2 5.2 %shard_map.39 = bf16[256,4096]{1,0:T(8,128)(2,1)} custom-call(f32[256,256]{1,0:T(8,128)S(1)} %get-tuple-element.9.base_ref, f32[256,256]{1,0:T(8,128)S(1)} %get-tuple-element.10.e_out_ref, bf16[8,128]{1,0:T(8,128)(2,1)S(1)} %slice.20.tail_ref, bf16[256,256]{1,0:T(8,128)(2,1)S(1)} %get-tuple-element.11.a_own_ref, bf16[256,256]{1,0:T(8,128)(2,1)S(1)} %shard_map.38.a_mate_ref, ...), custom_call_target="tpu_custom_call" | custom-call | tf_op jit(solution)/shard_map/pallas_call | solution.py:194
  (19 shorter events, 0.1 us)
Async XLA Ops:
  26.7 7.2 %collective-permute-start.2 = (bf16[32,4224]{1,0:T(8,128)(2,1)S(1)}, bf16[32,4224]{1,0:T(8,128)(2,1)S(1)}, u32[]{:S(2)}, u32[]{:S(2)}) collective-permute-start(bf16[32,4224]{1,0:T(8,128)(2,1)S(1)} %all_gather.3), channel_id=1, source_target_pairs={{0,1},{1,0},{2,3},{3,2},{4,5},{5,4},{6,7},{7,6},{8,9},{9,8},{10,11... | collective-permute-start | bytes 811016 | tf_op jit(solution)/shard_map/ppermute | solution.py:30
  33.9 17.6 %collective-permute-start.3 = (bf16[64,4224]{1,0:T(8,128)(2,1)S(1)}, bf16[64,4224]{1,0:T(8,128)(2,1)S(1)}, u32[]{:S(2)}, u32[]{:S(2)}) collective-permute-start(bf16[64,4224]{1,0:T(8,128)(2,1)S(1)} %constant_dynamic-update-slice_fusion.p1.refs_0_), channel_id=1, source_target_pairs={{2,0},{4,2},{6,4},{8,6},{10,8},{12,10},{14,12},{16,14},{18,16},{20... | collective-permute-start | bytes 1622024 | tf_op jit(solution)/shard_map/ppermute | solution.py:21
  37.8 48.8 %collective-permute-start = (bf16[256,4096]{1,0:T(8,128)(2,1)}, bf16[256,4096]{1,0:T(8,128)(2,1)S(1)}, u32[]{:S(2)}, u32[]{:S(2)}) collective-permute-start(bf16[256,4096]{1,0:T(8,128)(2,1)} %bitcast.6), channel_id=1, source_target_pairs={{0,32},{32,0},{1,33},{33,1},{2,34},{34,2},{3,35},{35,3},{4,36},{36... | collective-permute-start | bytes 6291464 | tf_op jit(solution)/shard_map/ppermute | solution.py:30
  44.3 48.1 %collective-permute-start.1 = (bf16[256,4096]{1,0:T(8,128)(2,1)}, bf16[256,4096]{1,0:T(8,128)(2,1)}, u32[]{:S(2)}, u32[]{:S(2)}) collective-permute-start(bf16[256,4096]{1,0:T(8,128)(2,1)} %bitcast.7), channel_id=1, source_target_pairs={{480,0},{64,32},{32,64},{128,96},{96,128},{192,160},{160,192},{256... | collective-permute-start | bytes 6291464 | tf_op jit(solution)/shard_map/ppermute | solution.py:36
  47.6 17.2 %collective-permute-start.4 = (bf16[64,4224]{1,0:T(8,128)(2,1)S(1)}, bf16[64,4224]{1,0:T(8,128)(2,1)S(1)}, u32[]{:S(2)}, u32[]{:S(2)}) collective-permute-start(bf16[64,4224]{1,0:T(8,128)(2,1)S(1)} %constant_dynamic-update-slice_fusion.p1.refs_0_), channel_id=1, source_target_pairs={{30,0},{0,2},{2,4},{4,6},{6,8},{8,10},{10,12},{12,14},{14,16},{16,... | collective-permute-start | bytes 1622024 | tf_op jit(solution)/shard_map/ppermute | solution.py:21
  49.6 17.4 %collective-permute-start.7 = (bf16[64,4224]{1,0:T(8,128)(2,1)S(1)}, bf16[64,4224]{1,0:T(8,128)(2,1)S(1)}, u32[]{:S(2)}, u32[]{:S(2)}) collective-permute-start(bf16[64,4224]{1,0:T(8,128)(2,1)S(1)} %constant_dynamic-update-slice_fusion.p1.refs_0_), channel_id=1, source_target_pairs={{0,32},{32,0},{1,33},{33,1},{2,34},{34,2},{3,35},{35,3},{4,36},{36... | collective-permute-start | bytes 1622024 | tf_op jit(solution)/shard_map/ppermute | solution.py:30
  51.5 29.8 %collective-permute-start.6 = (bf16[64,4224]{1,0:T(8,128)(2,1)S(1)}, bf16[64,4224]{1,0:T(8,128)(2,1)S(1)}, u32[]{:S(2)}, u32[]{:S(2)}) collective-permute-start(bf16[64,4224]{1,0:T(8,128)(2,1)S(1)} %constant_dynamic-update-slice_fusion.p1.refs_0_), channel_id=1, source_target_pairs={{480,0},{64,32},{32,64},{128,96},{96,128},{192,160},{160,192},{256... | collective-permute-start | bytes 1622024 | tf_op jit(solution)/shard_map/ppermute | solution.py:36
  57.7 34.8 %copy-start.1 = (bf16[256]{0:T(256)(128)(2,1)S(1)}, bf16[256]{0:T(256)(128)(2,1)}, u32[]{:S(2)}) copy-start(bf16[256]{0:T(256)(128)(2,1)} %param.5) | copy-start | bytes 1540
  57.7 34.8 %copy-start = (bf16[1,256,4096]{2,1,0:T(8,128)(2,1)S(1)}, bf16[1,256,4096]{2,1,0:T(8,128)(2,1)}, u32[]{:S(2)}) copy-start(bf16[1,256,4096]{2,1,0:T(8,128)(2,1)} %param.3) | copy-start | bytes 6291460
  65.0 19.5 %collective-permute-start.5 = (bf16[64,4224]{1,0:T(8,128)(2,1)S(1)}, bf16[64,4224]{1,0:T(8,128)(2,1)S(1)}, u32[]{:S(2)}, u32[]{:S(2)}) collective-permute-start(bf16[64,4224]{1,0:T(8,128)(2,1)S(1)} %get-tuple-element.13), channel_id=1, source_target_pairs={{30,0},{4,2},{2,4},{8,6},{6,8},{12,10},{10,12},{16,14},{14,16},{20... | collective-permute-start | bytes 1622024 | tf_op jit(solution)/shard_map/ppermute | solution.py:26
  67.0 29.5 %collective-permute-start.8 = (bf16[128,4224]{1,0:T(8,128)(2,1)S(1)}, bf16[128,4224]{1,0:T(8,128)(2,1)S(1)}, u32[]{:S(2)}, u32[]{:S(2)}) collective-permute-start(bf16[128,4224]{1,0:T(8,128)(2,1)S(1)} %get-tuple-element.14.p2.refs_1_), channel_id=1, source_target_pairs={{0,32},{32,0},{1,33},{33,1},{2,34},{34,2},{3,35},{35,3},{4,36},{36... | collective-permute-start | bytes 3244040 | tf_op jit(solution)/shard_map/ppermute | solution.py:30
  81.3 25.9 %collective-permute-start.10 = (bf16[128,4224]{1,0:T(8,128)(2,1)S(1)}, bf16[128,4224]{1,0:T(8,128)(2,1)S(1)}, u32[]{:S(2)}, u32[]{:S(2)}) collective-permute-start(bf16[128,4224]{1,0:T(8,128)(2,1)S(1)} %get-tuple-element.14.p2.refs_1_), channel_id=1, source_target_pairs={{480,0},{64,32},{32,64},{128,96},{96,128},{192,160},{160,192},{256... | collective-permute-start | bytes 3244040 | tf_op jit(solution)/shard_map/ppermute | solution.py:36
  84.6 11.9 %collective-permute-start.9 = (bf16[64,4224]{1,0:T(8,128)(2,1)S(1)}, bf16[64,4224]{1,0:T(8,128)(2,1)S(1)}, u32[]{:S(2)}, u32[]{:S(2)}) collective-permute-start(bf16[64,4224]{1,0:T(8,128)(2,1)S(1)} %collective-permute-done.5.p3.refs_2_), channel_id=1, source_target_pairs={{0,32},{32,0},{1,33},{33,1},{2,34},{34,2},{3,35},{35,3},{4,36},{36... | collective-permute-start | bytes 1622024 | tf_op jit(solution)/shard_map/ppermute | solution.py:30
  86.5 20.6 %collective-permute-start.11 = (bf16[64,4224]{1,0:T(8,128)(2,1)S(1)}, bf16[64,4224]{1,0:T(8,128)(2,1)S(1)}, u32[]{:S(2)}, u32[]{:S(2)}) collective-permute-start(bf16[64,4224]{1,0:T(8,128)(2,1)S(1)} %collective-permute-done.5.p3.refs_2_), channel_id=1, source_target_pairs={{480,0},{64,32},{32,64},{128,96},{96,128},{192,160},{160,192},{256... | collective-permute-start | bytes 1622024 | tf_op jit(solution)/shard_map/ppermute | solution.py:36

commit v3 on v2

--- a/solution.py
+++ b/solution.py
@@ -60,18 +60,12 @@
         copy.wait()
 
 
-def own_kernel(vir_ref, x_own, x_mate, x_out, p1, p2, p3, base_ref, a_own_ref, e_mate_ref, e_out_ref, xs, own, tails, sems):
+def own_kernel(vir_ref, x_own, x_mate, x_out, rows_own, base_ref, a_own_ref, e_mate_ref, e_out_ref, xs, own, tails, sems):
     width = own.shape[1]
-    pieces = gather_rows((p1, p2, p3), own, sems)
-    at = 0
-    for n, piece in enumerate((p1, p2, p3)):
-        copy = pltpu.make_async_copy(
-            piece.at[:, pl.ds(width, EXTRA)], tails.at[pl.ds(at, piece.shape[0]), :], sems.at[3 + n]
-        )
-        copy.start()
-        pieces.append(copy)
-        at += piece.shape[0]
-    blocks = [pltpu.make_async_copy(x, xs.at[n], sems.at[6 + n]) for n, x in enumerate((x_own, x_mate, x_out))]
+    pieces = gather_rows((rows_own,), own, sems)
+    pieces.append(pltpu.make_async_copy(rows_own.at[:, pl.ds(width, EXTRA)], tails, sems.at[1]))
+    pieces[1].start()
+    blocks = [pltpu.make_async_copy(x, xs.at[n], sems.at[2 + n]) for n, x in enumerate((x_own, x_mate, x_out))]
     for copy in blocks:
         copy.start()
     finish(pieces)
@@ -98,9 +92,9 @@
     return ((2.0 * contract(x_own, block) - exchange) / (base - energy)).astype(jnp.bfloat16)
 
 
-def mate_kernel(base_ref, e_mate_ref, tail_ref, x_own, c1, c2, c3, a_mate_ref, xs, mate, sems):
-    copies = gather_rows((c1, c2, c3), mate, sems)
-    block = pltpu.make_async_copy(x_own, xs, sems.at[3])
+def mate_kernel(base_ref, e_mate_ref, tail_ref, x_own, rows_mate, a_mate_ref, xs, mate, sems):
+    copies = gather_rows((rows_mate,), mate, sems)
+    block = pltpu.make_async_copy(x_own, xs, sems.at[1])
     block.start()
     finish(copies)
     block.wait()
@@ -111,10 +105,10 @@
 def density_kernel(base_ref, e_out_ref, tail_ref, a_own_ref, a_mate_ref, x_own, *refs):
     *pieces, out_ref, xs, rs, ds, sems = refs
     size = base_ref.shape[0]
-    out_copies = gather_rows(pieces[6:], rs, sems, 2 * size)
+    out_copies = gather_rows(pieces[2:], rs, sems, 2 * size)
     block = pltpu.make_async_copy(x_own, xs, sems.at[3])
     block.start()
-    others = gather_rows(pieces[:6], rs, sems.at[pl.ds(4, 6)])
+    others = gather_rows(pieces[:2], rs, sems.at[pl.ds(4, 2)])
     finish(out_copies)
     block.wait()
     energy = tail_ref[0:1, BATCH_DEV : BATCH_DEV + 1].astype(jnp.float32)
@@ -126,7 +120,7 @@
         width = xs.shape[1] // CHUNKS
         at = pl.ds(n * width, width)
         ds[:, at] = jnp.dot(amplitude, rs[:, at], preferred_element_type=jnp.float32).astype(jnp.bfloat16)
-        store = pltpu.make_async_copy(ds.at[:, at], out_ref.at[:, at], sems.at[10 + n])
+        store = pltpu.make_async_copy(ds.at[:, at], out_ref.at[:, at], sems.at[6 + n])
         store.start()
         stores.append(store)
     finish(stores)
@@ -147,21 +141,21 @@
     tail = jnp.concatenate([eps_vir[:BATCH_DEV], eps_occ, jnp.zeros(EXTRA - BATCH_DEV - 1, eps_vir.dtype)])
     slab = jnp.concatenate([x_own[:BATCH_DEV], jnp.broadcast_to(tail, (BATCH_DEV, EXTRA))], axis=1)
     part = lax.all_gather(slab, "zq", axis=0, tiled=True)
-    first = rows(part, swap(part, "xl"))
-    up, down = rotate(first, 1), rotate(first, -1)
+    part_x = swap(part, "xl")
+    even = lax.axis_index("zl") % 2 == 0
+    up, down = rotate(part, 1), rotate(part, -1)
+    up_x, down_x = rotate(part_x, 1), rotate(part_x, -1)
     x_mate = swap(x_own, "core")
-    y1 = outward(first)
-    c1 = swap(first, "core")
-    even = lax.axis_index("zl") % 2 == 0
-    third = pair_up(jnp.where(even, up, down))
-    second = rows(up, down)
-    y2 = outward(second)
-    c2 = swap(second, "core")
-    y3 = outward(third)
-    c3 = swap(third, "core")
-    own, mate, out = (first, second, third), (c1, c2, c3), (y1, y2, y3)
-
-    batch = sum(piece.shape[0] for piece in own)
+    y1 = outward(rows(part, part_x))
+    two = pair_up(jnp.where(even, up, down))
+    y2 = outward(rows(up, down, up_x, down_x))
+    two_x = pair_up(jnp.where(even, up_x, down_x))
+    y3 = outward(rows(two, two_x))
+    own = rows(part, part_x, up, down, up_x, down_x, two, two_x)
+    mate = swap(own, "core")
+    out = (y1, y2, y3)
+
+    batch = own.shape[0]
     pair_shape = (vir_dev, batch)
     wide = pltpu.VMEM((batch, aux), jnp.bfloat16)
     params = pltpu.CompilerParams(vmem_limit_bytes=24 << 20)
@@ -173,37 +167,37 @@
             jax.ShapeDtypeStruct(pair_shape, jnp.float32),
             jax.ShapeDtypeStruct(pair_shape, jnp.float32),
         ),
-        in_specs=[small()] + [large()] * 6,
+        in_specs=[small()] + [large()] * 4,
         out_specs=(small(),) * 4,
         scratch_shapes=[
             pltpu.VMEM((3, vir_dev, aux), jnp.bfloat16),
             wide,
             pltpu.VMEM((batch, EXTRA), jnp.bfloat16),
-            pltpu.SemaphoreType.DMA((9,)),
+            pltpu.SemaphoreType.DMA((5,)),
         ],
         compiler_params=params,
-    )(eps_vir.astype(jnp.float32)[None], x_own, x_mate, x_out, *own)
+    )(eps_vir.astype(jnp.float32)[None], x_own, x_mate, x_out, own)
     a_mate = pl.pallas_call(
         mate_kernel,
         out_shape=jax.ShapeDtypeStruct(pair_shape, jnp.bfloat16),
-        in_specs=[small()] * 3 + [large()] * 4,
+        in_specs=[small()] * 3 + [large()] * 2,
         out_specs=small(),
-        scratch_shapes=[pltpu.VMEM((vir_dev, aux), jnp.bfloat16), wide, pltpu.SemaphoreType.DMA((4,))],
+        scratch_shapes=[pltpu.VMEM((vir_dev, aux), jnp.bfloat16), wide, pltpu.SemaphoreType.DMA((2,))],
         compiler_params=params,
-    )(base, e_mate, c1[:BATCH_DEV, aux:], x_own, *mate)
+    )(base, e_mate, mate[:BATCH_DEV, aux:], x_own, mate)
     density = pl.pallas_call(
         density_kernel,
         out_shape=jax.ShapeDtypeStruct((vir_dev, aux), jnp.bfloat16),
-        in_specs=[small()] * 5 + [large()] * 10,
+        in_specs=[small()] * 5 + [large()] * 6,
         out_specs=large(),
         scratch_shapes=[
             pltpu.VMEM((vir_dev, aux), jnp.bfloat16),
             pltpu.VMEM((3 * batch, aux), jnp.bfloat16),
             pltpu.VMEM((vir_dev, aux), jnp.bfloat16),
-            pltpu.SemaphoreType.DMA((10 + CHUNKS,)),
+            pltpu.SemaphoreType.DMA((6 + CHUNKS,)),
         ],
         compiler_params=params,
-    )(base, e_out, y1[:BATCH_DEV, aux:], a_own, a_mate, x_own, *own, *mate, *out)
+    )(base, e_out, y1[:BATCH_DEV, aux:], a_own, a_mate, x_own, own, mate, *out)
     return density[None]
 
 

time: 113 us -> 123 us (1.088)
  the two profiles are of different devices: /device:TPU:27 before, /device:TPU:2 now
where the time goes in v3:
time: 123 us
  starting transfers between devices  41.4 us (34%)
  waiting for transfers between devices  39.2 us (32%)
  blocking collectives  28.6 us (23%)
  Pallas kernels  10.7 us (9%)
    all_gather x1, blocking collectives, shards(): part = lax.all_gather(slab, 'zq', axis=0, tiled=True)  28.6 us
    ppermute x4, starting transfers between devices, outward(): return lax.ppermute(block, OCC, route)  17.7 us
    ppermute x4, waiting for transfers between devices, rotate(): lax.ppermute(block, Z, [((i + distance) % size, i) for i in range(size)])  16.7 us
    ppermute x4, waiting for transfers between devices, outward(): return lax.ppermute(block, OCC, route)  14.8 us
    ppermute x4, starting transfers between devices, rotate(): lax.ppermute(block, Z, [((i + distance) % size, i) for i in range(size)])  13.5 us
    ppermute x2, waiting for transfers between devices, pair_up(): lax.ppermute(block, Z, [((i + 1 if i % 2 else i - 1) % size, i) for i in...  7.6 us
    ppermute x3, starting transfers between devices, swap(): return lax.ppermute(block, axis, [(0, 1), (1, 0)])  6.34 us
    pallas_call x1, Pallas kernels, shards(): pl.pallas_call(density_kernel, out_shape=jax.ShapeDtypeStruct((vir_dev, a...  5.21 us
  transfers between devices with their start and end apart: 13, of which 5 were waited for; matrix products, arithmetic and copies ran while one was open for 2% of the time, Pallas kernels for 4%

profile of v3, /device:TPU:2, one launch (start us, length us, event | category | flops | bytes accessed | tf_op | source)
XLA Modules:
  0.0 122.9 jit_solution(17760752713000660876)
XLA Ops:
  0.0 1.9 %collective-permute-start = (bf16[256,4096]{1,0:T(8,128)(2,1)}, bf16[256,4096]{1,0:T(8,128)(2,1)}, u32[]{:S(2)}, u32[]{:S(2)}) collective-permute-start(bf16[256,4096]{1,0:T(8,128)(2,1)} %bitcast.6), channel_id=1, source_target_pairs={{0,32},{32,0},{1,33},{33,1},{2,34},{34,2},{3,35},{35,3},{4,36},{36... | collective-permute-start | bytes 6291464 | tf_op jit(solution)/shard_map/ppermute | solution.py:30
  1.9 6.6 %collective-permute-start.1 = (bf16[256,4096]{1,0:T(8,128)(2,1)}, bf16[256,4096]{1,0:T(8,128)(2,1)}, u32[]{:S(2)}, u32[]{:S(2)}) collective-permute-start(bf16[256,4096]{1,0:T(8,128)(2,1)} %bitcast.7), channel_id=1, source_target_pairs={{480,0},{64,32},{32,64},{128,96},{96,128},{192,160},{160,192},{256... | collective-permute-start | bytes 6291464 | tf_op jit(solution)/shard_map/ppermute | solution.py:36
  8.5 0.9 slice_bitcast_fusion
  10.0 0.7 pad_maximum_fusion.4
  10.8 28.6 %all_gather.3 = bf16[32,4224]{1,0:T(8,128)(2,1)S(1)} all-gather(bf16[8,4224]{1,0:T(8,128)(2,1)S(1)} %pad_maximum_fusion.3), channel_id=1, replica_groups=mesh['xh'=2,'y'=4,'core'=2,'zq'=4,'zl'=4,'xl'=2] {'zq'}, dimensions={0}, use_global_device_ids=true | all-gather | bytes 337920 | tf_op jit(solution)/shard_map/all_gather | solution.py:143
  39.4 2.4 %collective-permute-start.2 = (bf16[32,4224]{1,0:T(8,128)(2,1)S(1)}, bf16[32,4224]{1,0:T(8,128)(2,1)S(1)}, u32[]{:S(2)}, u32[]{:S(2)}) collective-permute-start(bf16[32,4224]{1,0:T(8,128)(2,1)S(1)} %all_gather.3), channel_id=1, source_target_pairs={{0,1},{1,0},{2,3},{3,2},{4,5},{5,4},{6,7},{7,6},{8,9},{9,8},{10,11... | collective-permute-start | bytes 811016 | tf_op jit(solution)/shard_map/ppermute | solution.py:30
  41.8 4.6 %collective-permute-start.3 = (bf16[32,4224]{1,0:T(8,128)(2,1)S(1)}, bf16[32,4224]{1,0:T(8,128)(2,1)S(1)}, u32[]{:S(2)}, u32[]{:S(2)}) collective-permute-start(bf16[32,4224]{1,0:T(8,128)(2,1)S(1)} %all_gather.3), channel_id=1, source_target_pairs={{2,0},{4,2},{6,4},{8,6},{10,8},{12,10},{14,12},{16,14},{18,16},{20... | collective-permute-start | bytes 811016 | tf_op jit(solution)/shard_map/ppermute | solution.py:21
  46.3 1.9 %collective-permute-start.4 = (bf16[32,4224]{1,0:T(8,128)(2,1)S(1)}, bf16[32,4224]{1,0:T(8,128)(2,1)S(1)}, u32[]{:S(2)}, u32[]{:S(2)}) collective-permute-start(bf16[32,4224]{1,0:T(8,128)(2,1)S(1)} %all_gather.3), channel_id=1, source_target_pairs={{30,0},{0,2},{2,4},{4,6},{6,8},{8,10},{10,12},{12,14},{14,16},{16,... | collective-permute-start | bytes 811016 | tf_op jit(solution)/shard_map/ppermute | solution.py:21
  48.3 5.1 %collective-permute-start.5 = (bf16[32,4224]{1,0:T(8,128)(2,1)S(1)}, bf16[32,4224]{1,0:T(8,128)(2,1)S(1)}, u32[]{:S(2)}, u32[]{:S(2)}) collective-permute-start(bf16[32,4224]{1,0:T(8,128)(2,1)S(1)} %collective-permute-done.2), channel_id=1, source_target_pairs={{2,0},{4,2},{6,4},{8,6},{10,8},{12,10},{14,12},{16,14},{18,16},{20... | collective-permute-start | bytes 811016 | tf_op jit(solution)/shard_map/ppermute | solution.py:21
  53.5 5.3 %collective-permute-done.4 = bf16[32,4224]{1,0:T(8,128)(2,1)S(1)} collective-permute-done((bf16[32,4224]{1,0:T(8,128)(2,1)S(1)}, bf16[32,4224]{1,0:T(8,128)(2,1)S(1)}, u32[]{:S(2)}, u32[]{:S(2)}) %collective-permute-start.4) | collective-permute-done | bytes 270368 | tf_op jit(solution)/shard_map/ppermute | solution.py:21
  58.9 1.9 %collective-permute-start.7 = (bf16[32,4224]{1,0:T(8,128)(2,1)S(1)}, bf16[32,4224]{1,0:T(8,128)(2,1)S(1)}, u32[]{:S(2)}, u32[]{:S(2)}) collective-permute-start(bf16[32,4224]{1,0:T(8,128)(2,1)S(1)} %get-tuple-element.15), channel_id=1, source_target_pairs={{30,0},{4,2},{2,4},{8,6},{6,8},{12,10},{10,12},{16,14},{14,16},{20... | collective-permute-start | bytes 811016 | tf_op jit(solution)/shard_map/ppermute | solution.py:26
  60.8 1.9 %collective-permute-start.6 = (bf16[32,4224]{1,0:T(8,128)(2,1)S(1)}, bf16[32,4224]{1,0:T(8,128)(2,1)S(1)}, u32[]{:S(2)}, u32[]{:S(2)}) collective-permute-start(bf16[32,4224]{1,0:T(8,128)(2,1)S(1)} %collective-permute-done.2), channel_id=1, source_target_pairs={{30,0},{0,2},{2,4},{4,6},{6,8},{8,10},{10,12},{12,14},{14,16},{16,... | collective-permute-start | bytes 811016 | tf_op jit(solution)/shard_map/ppermute | solution.py:21
  62.8 11.5 %collective-permute-done.6 = bf16[32,4224]{1,0:T(8,128)(2,1)S(1)} collective-permute-done((bf16[32,4224]{1,0:T(8,128)(2,1)S(1)}, bf16[32,4224]{1,0:T(8,128)(2,1)S(1)}, u32[]{:S(2)}, u32[]{:S(2)}) %collective-permute-start.6) | collective-permute-done | bytes 270368 | tf_op jit(solution)/shard_map/ppermute | solution.py:21
  74.3 1.9 %collective-permute-start.8 = (bf16[32,4224]{1,0:T(8,128)(2,1)S(1)}, bf16[32,4224]{1,0:T(8,128)(2,1)S(1)}, u32[]{:S(2)}, u32[]{:S(2)}) collective-permute-start(bf16[32,4224]{1,0:T(8,128)(2,1)S(1)} %get-tuple-element.13), channel_id=1, source_target_pairs={{30,0},{4,2},{2,4},{8,6},{6,8},{12,10},{10,12},{16,14},{14,16},{20... | collective-permute-start | bytes 811016 | tf_op jit(solution)/shard_map/ppermute | solution.py:26
  76.3 7.6 %collective-permute-done.8 = bf16[32,4224]{1,0:T(8,128)(2,1)S(1)} collective-permute-done((bf16[32,4224]{1,0:T(8,128)(2,1)S(1)}, bf16[32,4224]{1,0:T(8,128)(2,1)S(1)}, u32[]{:S(2)}, u32[]{:S(2)}) %collective-permute-start.8) | collective-permute-done | bytes 270368 | tf_op jit(solution)/shard_map/ppermute | solution.py:26
  83.9 2.1 %collective-permute-start.10 = (bf16[256,4224]{1,0:T(8,128)(2,1)S(1)}, bf16[256,4224]{1,0:T(8,128)(2,1)S(1)}, u32[]{:S(2)}, u32[]{:S(2)}) collective-permute-start(bf16[256,4224]{1,0:T(8,128)(2,1)S(1)} %constant_dynamic-update-slice_fusion.rows_own.refs_0_), channel_id=1, source_target_pairs={{0,32},{32,0},{1,33},{33,1},{2,34},{34,2},{3,35},{35,3},{4,36},{36... | collective-permute-start | bytes 6488072 | tf_op jit(solution)/shard_map/ppermute | solution.py:30
  86.0 1.9 %collective-permute-start.9 = (bf16[64,4224]{1,0:T(8,128)(2,1)S(1)}, bf16[64,4224]{1,0:T(8,128)(2,1)S(1)}, u32[]{:S(2)}, u32[]{:S(2)}) collective-permute-start(bf16[64,4224]{1,0:T(8,128)(2,1)S(1)} %pad_maximum_fusion.1), channel_id=1, source_target_pairs={{480,0},{64,32},{32,64},{128,96},{96,128},{192,160},{160,192},{256... | collective-permute-start | bytes 1622024 | tf_op jit(solution)/shard_map/ppermute | solution.py:36
  88.1 7.3 %collective-permute-start.11 = (bf16[128,4224]{1,0:T(8,128)(2,1)S(1)}, bf16[128,4224]{1,0:T(8,128)(2,1)S(1)}, u32[]{:S(2)}, u32[]{:S(2)}) collective-permute-start(bf16[128,4224]{1,0:T(8,128)(2,1)S(1)} %pad_maximum_fusion), channel_id=1, source_target_pairs={{480,0},{64,32},{32,64},{128,96},{96,128},{192,160},{160,192},{256... | collective-permute-start | bytes 3244040 | tf_op jit(solution)/shard_map/ppermute | solution.py:36
  95.4 5.0 %collective-permute-done.9.refs_2_ = bf16[64,4224]{1,0:T(8,128)(2,1)S(1)} collective-permute-done((bf16[64,4224]{1,0:T(8,128)(2,1)S(1)}, bf16[64,4224]{1,0:T(8,128)(2,1)S(1)}, u32[]{:S(2)}, u32[]{:S(2)}) %collective-permute-start.9) | collective-permute-done | bytes 540704 | tf_op jit(solution)/shard_map/ppermute | solution.py:36
  100.3 1.9 %collective-permute-start.12 = (bf16[64,4224]{1,0:T(8,128)(2,1)S(1)}, bf16[64,4224]{1,0:T(8,128)(2,1)S(1)}, u32[]{:S(2)}, u32[]{:S(2)}) collective-permute-start(bf16[64,4224]{1,0:T(8,128)(2,1)S(1)} %pad_maximum_fusion.2), channel_id=1, source_target_pairs={{480,0},{64,32},{32,64},{128,96},{96,128},{192,160},{160,192},{256... | collective-permute-start | bytes 1622024 | tf_op jit(solution)/shard_map/ppermute | solution.py:36
  102.3 4.4 %shard_map.37 = (f32[256,256]{1,0:T(8,128)S(1)}, bf16[256,256]{1,0:T(8,128)(2,1)S(1)}, f32[256,256]{1,0:T(8,128)S(1)}, f32[256,256]{1,0:T(8,128)S(1)}) custom-call(f32[1,256]{1,0:T(1,128)S(1)} %bitcast.11, bf16[256,4096]{1,0:T(8,128)(2,1)S(1)} %bitcast.8, bf16[256,4096]{1,0:T(8,128)(2,1)} %collective-permute-done.x_mate, ...), custom_call_target="tpu_custom_call" | custom-call | tf_op jit(solution)/shard_map/pallas_call | solution.py:162
  106.8 1.1 shard_map.38.a_mate_ref
  107.8 9.9 %collective-permute-done.12.refs_4_ = bf16[64,4224]{1,0:T(8,128)(2,1)S(1)} collective-permute-done((bf16[64,4224]{1,0:T(8,128)(2,1)S(1)}, bf16[64,4224]{1,0:T(8,128)(2,1)S(1)}, u32[]{:S(2)}, u32[]{:S(2)}) %collective-permute-start.12) | collective-permute-done | bytes 540704 | tf_op jit(solution)/shard_map/ppermute | solution.py:36
  117.7 5.2 %shard_map.39 = bf16[256,4096]{1,0:T(8,128)(2,1)} custom-call(f32[256,256]{1,0:T(8,128)S(1)} %get-tuple-element.9.base_ref, f32[256,256]{1,0:T(8,128)S(1)} %get-tuple-element.10.e_out_ref, bf16[8,128]{1,0:T(8,128)(2,1)S(1)} %slice.20.tail_ref, bf16[256,256]{1,0:T(8,128)(2,1)S(1)} %get-tuple-element.11.a_own_ref, bf16[256,256]{1,0:T(8,128)(2,1)S(1)} %shard_map.38.a_mate_ref, ...), custom_call_target="tpu_custom_call" | custom-call | tf_op jit(solution)/shard_map/pallas_call | solution.py:188
  (28 shorter events, 0.5 us)
Async XLA Ops:
  0.0 102.3 %collective-permute-start = (bf16[256,4096]{1,0:T(8,128)(2,1)}, bf16[256,4096]{1,0:T(8,128)(2,1)}, u32[]{:S(2)}, u32[]{:S(2)}) collective-permute-start(bf16[256,4096]{1,0:T(8,128)(2,1)} %bitcast.6), channel_id=1, source_target_pairs={{0,32},{32,0},{1,33},{33,1},{2,34},{34,2},{3,35},{35,3},{4,36},{36... | collective-permute-start | bytes 6291464 | tf_op jit(solution)/shard_map/ppermute | solution.py:30
  1.9 100.4 %collective-permute-start.1 = (bf16[256,4096]{1,0:T(8,128)(2,1)}, bf16[256,4096]{1,0:T(8,128)(2,1)}, u32[]{:S(2)}, u32[]{:S(2)}) collective-permute-start(bf16[256,4096]{1,0:T(8,128)(2,1)} %bitcast.7), channel_id=1, source_target_pairs={{480,0},{64,32},{32,64},{128,96},{96,128},{192,160},{160,192},{256... | collective-permute-start | bytes 6291464 | tf_op jit(solution)/shard_map/ppermute | solution.py:36
  39.4 8.9 %collective-permute-start.2 = (bf16[32,4224]{1,0:T(8,128)(2,1)S(1)}, bf16[32,4224]{1,0:T(8,128)(2,1)S(1)}, u32[]{:S(2)}, u32[]{:S(2)}) collective-permute-start(bf16[32,4224]{1,0:T(8,128)(2,1)S(1)} %all_gather.3), channel_id=1, source_target_pairs={{0,1},{1,0},{2,3},{3,2},{4,5},{5,4},{6,7},{7,6},{8,9},{9,8},{10,11... | collective-permute-start | bytes 811016 | tf_op jit(solution)/shard_map/ppermute | solution.py:30
  41.8 11.7 %collective-permute-start.3 = (bf16[32,4224]{1,0:T(8,128)(2,1)S(1)}, bf16[32,4224]{1,0:T(8,128)(2,1)S(1)}, u32[]{:S(2)}, u32[]{:S(2)}) collective-permute-start(bf16[32,4224]{1,0:T(8,128)(2,1)S(1)} %all_gather.3), channel_id=1, source_target_pairs={{2,0},{4,2},{6,4},{8,6},{10,8},{12,10},{14,12},{16,14},{18,16},{20... | collective-permute-start | bytes 811016 | tf_op jit(solution)/shard_map/ppermute | solution.py:21
  46.3 12.5 %collective-permute-start.4 = (bf16[32,4224]{1,0:T(8,128)(2,1)S(1)}, bf16[32,4224]{1,0:T(8,128)(2,1)S(1)}, u32[]{:S(2)}, u32[]{:S(2)}) collective-permute-start(bf16[32,4224]{1,0:T(8,128)(2,1)S(1)} %all_gather.3), channel_id=1, source_target_pairs={{30,0},{0,2},{2,4},{4,6},{6,8},{8,10},{10,12},{12,14},{14,16},{16,... | collective-permute-start | bytes 811016 | tf_op jit(solution)/shard_map/ppermute | solution.py:21
  48.3 14.4 %collective-permute-start.5 = (bf16[32,4224]{1,0:T(8,128)(2,1)S(1)}, bf16[32,4224]{1,0:T(8,128)(2,1)S(1)}, u32[]{:S(2)}, u32[]{:S(2)}) collective-permute-start(bf16[32,4224]{1,0:T(8,128)(2,1)S(1)} %collective-permute-done.2), channel_id=1, source_target_pairs={{2,0},{4,2},{6,4},{8,6},{10,8},{12,10},{14,12},{16,14},{18,16},{20... | collective-permute-start | bytes 811016 | tf_op jit(solution)/shard_map/ppermute | solution.py:21
  58.9 17.4 %collective-permute-start.7 = (bf16[32,4224]{1,0:T(8,128)(2,1)S(1)}, bf16[32,4224]{1,0:T(8,128)(2,1)S(1)}, u32[]{:S(2)}, u32[]{:S(2)}) collective-permute-start(bf16[32,4224]{1,0:T(8,128)(2,1)S(1)} %get-tuple-element.15), channel_id=1, source_target_pairs={{30,0},{4,2},{2,4},{8,6},{6,8},{12,10},{10,12},{16,14},{14,16},{20... | collective-permute-start | bytes 811016 | tf_op jit(solution)/shard_map/ppermute | solution.py:26
  60.8 13.4 %collective-permute-start.6 = (bf16[32,4224]{1,0:T(8,128)(2,1)S(1)}, bf16[32,4224]{1,0:T(8,128)(2,1)S(1)}, u32[]{:S(2)}, u32[]{:S(2)}) collective-permute-start(bf16[32,4224]{1,0:T(8,128)(2,1)S(1)} %collective-permute-done.2), channel_id=1, source_target_pairs={{30,0},{0,2},{2,4},{4,6},{6,8},{8,10},{10,12},{12,14},{14,16},{16,... | collective-permute-start | bytes 811016 | tf_op jit(solution)/shard_map/ppermute | solution.py:21
  74.3 9.6 %collective-permute-start.8 = (bf16[32,4224]{1,0:T(8,128)(2,1)S(1)}, bf16[32,4224]{1,0:T(8,128)(2,1)S(1)}, u32[]{:S(2)}, u32[]{:S(2)}) collective-permute-start(bf16[32,4224]{1,0:T(8,128)(2,1)S(1)} %get-tuple-element.13), channel_id=1, source_target_pairs={{30,0},{4,2},{2,4},{8,6},{6,8},{12,10},{10,12},{16,14},{14,16},{20... | collective-permute-start | bytes 811016 | tf_op jit(solution)/shard_map/ppermute | solution.py:26
  83.9 18.3 %copy-start.1 = (bf16[256]{0:T(256)(128)(2,1)S(1)}, bf16[256]{0:T(256)(128)(2,1)}, u32[]{:S(2)}) copy-start(bf16[256]{0:T(256)(128)(2,1)} %param.5) | copy-start | bytes 1540
  83.9 18.4 %copy-start = (bf16[1,256,4096]{2,1,0:T(8,128)(2,1)S(1)}, bf16[1,256,4096]{2,1,0:T(8,128)(2,1)}, u32[]{:S(2)}) copy-start(bf16[1,256,4096]{2,1,0:T(8,128)(2,1)} %param.3) | copy-start | bytes 6291460
  83.9 22.8 %collective-permute-start.10 = (bf16[256,4224]{1,0:T(8,128)(2,1)S(1)}, bf16[256,4224]{1,0:T(8,128)(2,1)S(1)}, u32[]{:S(2)}, u32[]{:S(2)}) collective-permute-start(bf16[256,4224]{1,0:T(8,128)(2,1)S(1)} %constant_dynamic-update-slice_fusion.rows_own.refs_0_), channel_id=1, source_target_pairs={{0,32},{32,0},{1,33},{33,1},{2,34},{34,2},{3,35},{35,3},{4,36},{36... | collective-permute-start | bytes 6488072 | tf_op jit(solution)/shard_map/ppermute | solution.py:30
  86.0 14.3 %collective-permute-start.9 = (bf16[64,4224]{1,0:T(8,128)(2,1)S(1)}, bf16[64,4224]{1,0:T(8,128)(2,1)S(1)}, u32[]{:S(2)}, u32[]{:S(2)}) collective-permute-start(bf16[64,4224]{1,0:T(8,128)(2,1)S(1)} %pad_maximum_fusion.1), channel_id=1, source_target_pairs={{480,0},{64,32},{32,64},{128,96},{96,128},{192,160},{160,192},{256... | collective-permute-start | bytes 1622024 | tf_op jit(solution)/shard_map/ppermute | solution.py:36
  88.1 29.7 %collective-permute-start.11 = (bf16[128,4224]{1,0:T(8,128)(2,1)S(1)}, bf16[128,4224]{1,0:T(8,128)(2,1)S(1)}, u32[]{:S(2)}, u32[]{:S(2)}) collective-permute-start(bf16[128,4224]{1,0:T(8,128)(2,1)S(1)} %pad_maximum_fusion), channel_id=1, source_target_pairs={{480,0},{64,32},{32,64},{128,96},{96,128},{192,160},{160,192},{256... | collective-permute-start | bytes 3244040 | tf_op jit(solution)/shard_map/ppermute | solution.py:36
  100.3 17.4 %collective-permute-start.12 = (bf16[64,4224]{1,0:T(8,128)(2,1)S(1)}, bf16[64,4224]{1,0:T(8,128)(2,1)S(1)}, u32[]{:S(2)}, u32[]{:S(2)}) collective-permute-start(bf16[64,4224]{1,0:T(8,128)(2,1)S(1)} %pad_maximum_fusion.2), channel_id=1, source_target_pairs={{480,0},{64,32},{32,64},{128,96},{96,128},{192,160},{160,192},{256... | collective-permute-start | bytes 1622024 | tf_op jit(solution)/shard_map/ppermute | solution.py:36
